TPU v7x, 32 devices: a whole 2x2x4 slice. The times are simulated.
32 devices in a mesh: depth: 2 (over core), seq: 16 (over z, y, x).
Axes of the slice: x: 2, y: 2, z: 4, core: 2. Of those that a mesh axis runs over, the one named last changes fastest.
Arguments:
- queries: bfloat16 [2, 2048, 4096], P('depth', 'seq'), may hold values from -27 to 27
- grad_out: bfloat16 [2, 2048, 4096], P('depth', 'seq'), may hold values from -48 to 48
- key_states: bfloat16 [2048, 4096], P('depth', 'seq'), may hold values from -3 to 3
- value_states: bfloat16 [2048, 4096], P('depth', 'seq'), may hold values from -6 to 6
- offsets: int32 [2], replicated, may hold values from 0 to 8, as said below
- windows: int32 [2], replicated, may hold values from 512 to 1024, as said below
Outputs:
- grad_queries: bfloat16 [2, 2048, 4096], P('depth', 'seq')
- grad_keys: bfloat16 [2048, 4096], P('depth', 'seq')
- grad_values: bfloat16 [2048, 4096], P('depth', 'seq')
Inputs may be any that keep to these rules, and one draw needn't show every extreme that they name: `windows`: one depth's window is exactly 1024. `offsets`: one depth's offset is exactly 8.
All inputs are finite; a program needn't handle non-finite values.
Results may differ from a plain program's by a relative error of at most 0.033.
Values may be sent and summed in bfloat16 or wider, within the bound.
No kernel may reach another device: no remote copies, remote signals or barrier semaphores. Data moves between devices by JAX's collectives and lax.ppermute only.
A program may use at most 64 MiB of HBM per device.

v0:
```python
import functools
import math

import jax
import jax.numpy as jnp
from jax import lax
from jax.experimental import pallas as pl
from jax.experimental.pallas import tpu as pltpu
from jax.sharding import PartitionSpec as P


HEAD_DIM = 128
WIN = 1024
EDGE = 16
SCALING = 1.0 / math.sqrt(HEAD_DIM)
EXP2_SCALE = SCALING * math.log2(math.e)
LOWEST = -1e30


def nt_dot(a, b):
    return lax.dot_general(a, b, (((1,), (1,)), ((), ())), preferred_element_type=jnp.float32)


def nn_dot(a, b):
    return lax.dot_general(a, b, (((1,), (0,)), ((), ())), preferred_element_type=jnp.float32)


def backward_kernel(block, past, n_blocks, head, n_pieces, n_parts, *refs):
    offsets_ref, windows_ref, *refs = refs
    pieces, refs = refs[:n_pieces], refs[n_pieces:]
    key_parts, refs = refs[:n_parts], refs[n_parts:]
    value_parts, refs = refs[:n_parts], refs[n_parts:]
    dq_ref, *refs = refs
    sums, refs = refs[:n_parts], refs[n_parts:]
    held_ref, k_ref, v_ref, kt_ref, bias_ref, p_ref, gp_ref, dk_acc, dv_acc, sems = refs

    number = pl.program_id(0)
    depth_id, seq_id = lax.axis_index("depth"), lax.axis_index("seq")
    shift = offsets_ref[depth_id]
    span = windows_ref[depth_id]
    seq_total = n_blocks * block
    part_rows = seq_total // n_parts
    tok_rows = held_ref.shape[2]

    def part_at(n):
        return pl.ds(pl.multiple_of((depth_id ^ n) * part_rows, part_rows) if n_parts > 1 else 0, part_rows)

    @pl.when(number == 0)
    def _():
        columns = pl.ds(head * HEAD_DIM, HEAD_DIM)
        copies = []
        for n in range(n_parts):
            for parts, ref in ((key_parts, k_ref), (value_parts, v_ref)):
                copies.append((parts[n].at[:, columns], ref.at[part_at(n)]))
        for k in range(n_pieces):
            copies.append((pieces[k], held_ref.at[seq_id ^ k] if n_pieces > 1 else held_ref))
        copies = [
            pltpu.make_async_copy(source, target, sems.at[n])
            for n, (source, target) in enumerate(copies)
        ]
        for copy in copies:
            copy.start()
        dk_acc[...] = jnp.zeros_like(dk_acc)
        dv_acc[...] = jnp.zeros_like(dv_acc)
        ahead = lax.broadcasted_iota(jnp.int32, (8, block), 0) - lax.broadcasted_iota(
            jnp.int32, (8, block), 1
        )
        for back in range(past + 1):
            for row in range(0, block, 8):
                lead = row - back * block
                keep = ahead > shift - span - lead
                if lead + 7 > 0:
                    keep = keep & (ahead <= shift - lead)
                bias_ref[back, pl.ds(row, 8), :] = jnp.where(keep, 0.0, -jnp.inf)
        for copy in copies:
            copy.wait()
        kt_ref[...] = k_ref[...].T

    def step(n_past):
        first_row = pl.multiple_of(number * block, block)
        per_block = block // tok_rows
        held = pl.ds(number * per_block, per_block)
        query = held_ref[held, 0].reshape(block, HEAD_DIM)
        grad = held_ref[held, 1].reshape(block, HEAD_DIM)
        edge_first = pl.multiple_of(jnp.minimum(first_row + block, seq_total - EDGE), EDGE)
        edge_key = edge_first + lax.broadcasted_iota(jnp.int32, (EDGE, block), 0)
        edge_query = first_row + lax.broadcasted_iota(jnp.int32, (EDGE, block), 1)
        edge_in = (edge_key >= first_row + block) & (edge_key - edge_query <= shift)
        tiles = [
            (pl.multiple_of((number - back) * block, block), block, back * block, back)
            for back in range(n_past + 1)
        ]
        tiles.append((edge_first, EDGE, (past + 1) * block, None))

        highest = jnp.full((1, block), LOWEST, jnp.float32)
        total = jnp.zeros((1, block), jnp.float32)
        dotted = jnp.zeros((1, block), jnp.float32)
        highs = []
        for key_first, rows, at, back in tiles:
            score = nt_dot(k_ref[pl.ds(key_first, rows), :], query)
            if back is None:
                score = jnp.where(edge_in, score, -jnp.inf)
            else:
                score = score + bias_ref[back]
            now = jnp.maximum(highest, jnp.max(score, axis=0, keepdims=True))
            part = jnp.exp2((score - now) * EXP2_SCALE)
            grad_prob = nt_dot(v_ref[pl.ds(key_first, rows), :], grad)
            p_ref[pl.ds(at, rows), :] = part
            gp_ref[pl.ds(at, rows), :] = grad_prob
            less = jnp.exp2((highest - now) * EXP2_SCALE)
            total = total * less + jnp.sum(part, axis=0, keepdims=True)
            dotted = dotted * less + jnp.sum(part * grad_prob, axis=0, keepdims=True)
            highest = now
            highs.append(now)
        inverse = 1.0 / total
        row_dot = dotted * inverse

        dq_t = jnp.zeros((HEAD_DIM, block), jnp.float32)
        for (key_first, rows, at, back), high in zip(tiles, highs, strict=True):
            prob = p_ref[pl.ds(at, rows), :] * (inverse * jnp.exp2((high - highest) * EXP2_SCALE))
            weight = prob.astype(jnp.bfloat16)
            grad_score = (prob * (gp_ref[pl.ds(at, rows), :] - row_dot)).astype(jnp.bfloat16)
            here = pl.ds(key_first, rows)
            dv_acc[here, :] += nn_dot(weight, grad)
            dk_acc[here, :] += nn_dot(grad_score, query)
            if back is None:
                dq_t = dq_t + lax.dot_general(
                    k_ref[here, :], grad_score, (((0,), (0,)), ((), ())),
                    preferred_element_type=jnp.float32,
                )
            else:
                dq_t = dq_t + nn_dot(kt_ref[:, here], grad_score)
        dq_ref[...] = (dq_t * SCALING).T.astype(jnp.bfloat16).reshape(dq_ref.shape)

    for n_past in range(past):
        pl.when(number == n_past)(functools.partial(step, n_past))
    pl.when(number >= past)(functools.partial(step, past))

    @pl.when(number == n_blocks - 1)
    def _():
        for n in range(n_parts):
            sums[n][0] = (dk_acc[part_at(n), :] * SCALING).astype(jnp.bfloat16)
            sums[n][1] = dv_acc[part_at(n), :].astype(jnp.bfloat16)


def attention_backward(offsets, windows, pieces, key_parts, value_parts, head):
    n_pieces, n_parts = len(pieces), len(key_parts)
    tok_rows = pieces[0].shape[-2]
    seq_total = key_parts[0].shape[0] * n_parts
    sources = seq_total // tok_rows
    block = min(2 * tok_rows, seq_total)
    per_block = block // tok_rows
    n_blocks = seq_total // block
    past = min(-(-WIN // block), n_blocks - 1)
    rows = (past + 1) * block + EDGE
    pairs = seq_total * rows
    f32, bf16 = jnp.float32, jnp.bfloat16
    sums_shape = (2, seq_total // n_parts, HEAD_DIM)
    dq, *sums = pl.pallas_call(
        functools.partial(backward_kernel, block, past, n_blocks, head, n_pieces, n_parts),
        grid_spec=pltpu.PrefetchScalarGridSpec(
            num_scalar_prefetch=2,
            grid=(n_blocks,),
            in_specs=[pl.BlockSpec(memory_space=pl.ANY)] * (n_pieces + 2 * n_parts),
            out_specs=[pl.BlockSpec((per_block, tok_rows, HEAD_DIM), lambda i, *_: (i, 0, 0))]
            + [pl.BlockSpec(sums_shape, lambda i, *_: (0, 0, 0))] * n_parts,
            scratch_shapes=[
                pltpu.VMEM((sources, 2, tok_rows, HEAD_DIM), bf16),
                pltpu.VMEM((seq_total, HEAD_DIM), bf16),
                pltpu.VMEM((seq_total, HEAD_DIM), bf16),
                pltpu.VMEM((HEAD_DIM, seq_total), bf16),
                pltpu.VMEM((past + 1, block, block), f32),
                pltpu.VMEM((rows, block), f32),
                pltpu.VMEM((rows, block), f32),
                pltpu.VMEM((seq_total, HEAD_DIM), f32),
                pltpu.VMEM((seq_total, HEAD_DIM), f32),
                pltpu.SemaphoreType.DMA((n_pieces + 2 * n_parts,)),
            ],
        ),
        out_shape=[jax.ShapeDtypeStruct((sources, tok_rows, HEAD_DIM), bf16)]
        + [jax.ShapeDtypeStruct(sums_shape, bf16)] * n_parts,
        cost_estimate=pl.CostEstimate(
            flops=10 * pairs * HEAD_DIM, bytes_accessed=14 * seq_total * HEAD_DIM, transcendentals=pairs
        ),
    )(offsets, windows, *pieces, *key_parts, *value_parts)
    return dq, sums


def pack(head, heads, queries, grad_out, n_outs):
    tok_rows, model_width = queries.shape
    parts = model_width // (heads * HEAD_DIM)
    shape = (2, tok_rows, HEAD_DIM)

    def kernel(q_ref, g_ref, *refs):
        outs, (held, in_sems, out_sems) = refs[:n_outs], refs[n_outs:]
        seq_id = lax.axis_index("seq")
        loads, stores = [], []
        for k in range(parts):
            dest = seq_id ^ k if n_outs > 1 else k
            start = pl.multiple_of((dest * heads + head) * HEAD_DIM, HEAD_DIM)
            for a, ref in enumerate((q_ref, g_ref)):
                loads.append(
                    pltpu.make_async_copy(
                        ref.at[:, pl.ds(start, HEAD_DIM)], held.at[k, a], in_sems.at[k, a]
                    )
                )
            target = outs[k] if n_outs > 1 else outs[0].at[k]
            stores.append(pltpu.make_async_copy(held.at[k], target, out_sems.at[k]))
        for load in loads:
            load.start()
        for k in range(parts):
            loads[2 * k].wait()
            loads[2 * k + 1].wait()
            stores[k].start()
        for store in stores:
            store.wait()

    return pl.pallas_call(
        kernel,
        in_specs=[pl.BlockSpec(memory_space=pl.ANY)] * 2,
        out_specs=[pl.BlockSpec(memory_space=pl.ANY)] * n_outs,
        out_shape=[jax.ShapeDtypeStruct(shape if n_outs > 1 else (parts, *shape), jnp.bfloat16)] * n_outs,
        scratch_shapes=[
            pltpu.VMEM((parts, *shape), jnp.bfloat16),
            pltpu.SemaphoreType.DMA((parts, 2)),
            pltpu.SemaphoreType.DMA((parts,)),
        ],
        cost_estimate=pl.CostEstimate(
            flops=0, bytes_accessed=4 * parts * math.prod(shape), transcendentals=0
        ),
    )(queries, grad_out)


def unpack(back, tok_rows, model_width):
    heads = len(back)
    parts = back[0].shape[0]

    def kernel(*refs):
        ins, out, sems = refs[:heads], refs[heads], refs[heads + 1]
        copies = []
        for head in range(heads):
            for d in range(parts):
                columns = pl.ds((d * heads + head) * HEAD_DIM, HEAD_DIM)
                copies.append(
                    pltpu.make_async_copy(ins[head].at[d], out.at[:, columns], sems.at[head, d])
                )
        for copy in copies:
            copy.start()
        for copy in copies:
            copy.wait()

    return pl.pallas_call(
        kernel,
        in_specs=[pl.BlockSpec(memory_space=pl.ANY)] * heads,
        out_specs=pl.BlockSpec(memory_space=pltpu.VMEM),
        out_shape=jax.ShapeDtypeStruct((tok_rows, model_width), jnp.bfloat16),
        scratch_shapes=[pltpu.SemaphoreType.DMA((heads, parts))],
        compiler_params=pltpu.CompilerParams(vmem_limit_bytes=8 * 2**20),
        name="unpack",
    )(*back)


def on_device(queries, grad_out, key_states, value_states, offsets, windows):
    depths = lax.axis_size("depth")
    parts = lax.axis_size("seq")
    tok_rows, model_width = queries.shape[1:]
    heads = key_states.shape[1] // HEAD_DIM
    queries = queries.reshape(tok_rows, model_width)
    grad_out = grad_out.reshape(tok_rows, model_width)

    def received(head):
        if head + 1 < heads and parts & (parts - 1) == 0:
            sent = pack(head, heads, queries, grad_out, parts)
            landed = [sent[0]]
            for k in range(1, parts):
                landed.append(lax.ppermute(sent[k], "seq", [(i, i ^ k) for i in range(parts)]))
            return landed
        (sent,) = pack(head, heads, queries, grad_out, 1)
        return [lax.all_to_all(sent, "seq", split_axis=0, concat_axis=0, tiled=True)]

    pieces = [received(head) for head in range(heads)]

    swap = [(0, 1), (1, 0)]
    if depths == 2:
        key_parts = [key_states, lax.ppermute(key_states, "depth", swap)]
        value_parts = [value_states, lax.ppermute(value_states, "depth", swap)]
    else:
        key_parts = [lax.all_gather(key_states, "depth", axis=0, tiled=True)]
        value_parts = [lax.all_gather(value_states, "depth", axis=0, tiled=True)]

    def over_depths(sums):
        if depths == 2:
            other = lax.ppermute(sums[1], "depth", swap)
            return (sums[0].astype(jnp.float32) + other.astype(jnp.float32)).astype(jnp.bfloat16)
        return lax.psum_scatter(sums[0], "depth", scatter_dimension=1, tiled=True)

    back, totals = [], []
    for head in range(heads):
        dq, sums = attention_backward(offsets, windows, pieces[head], key_parts, value_parts, head)
        back.append(lax.all_to_all(dq, "seq", split_axis=0, concat_axis=0, tiled=True))
        totals.append(over_depths(sums))

    return (
        unpack(back, tok_rows, model_width).reshape(1, tok_rows, model_width),
        jnp.concatenate([total[0] for total in totals], axis=1),
        jnp.concatenate([total[1] for total in totals], axis=1),
    )


def solution(mesh):
    in_specs = (
        P("depth", "seq", None),
        P("depth", "seq", None),
        P("depth", "seq"),
        P("depth", "seq"),
        P(),
        P(),
    )
    out_specs = (P("depth", "seq", None), P("depth", "seq"), P("depth", "seq"))
    return jax.shard_map(
        on_device, mesh=mesh, in_specs=in_specs, out_specs=out_specs, check_vma=False
    )
```

profile of v0, /device:TPU:0, one launch (start us, length us, event | category | flops | bytes accessed | tf_op | source)
XLA Modules:
  0.0 119.7 jit_solution(18059157094455215036)
XLA Ops:
  0.6 2.2 %shard_map.87 = bf16[16,2,128,128]{3,2,1,0:T(8,128)(2,1)} custom-call(bf16[128,4096]{1,0:T(8,128)(2,1)} %bitcast.11, bf16[128,4096]{1,0:T(8,128)(2,1)} %bitcast.13), custom_call_target="tpu_custom_call" | custom-call | bytes 2097152 | tf_op jit(solution)/shard_map/pallas_call | solution.py:218
  2.9 0.0 copy-start.3
  2.9 0.0 copy-start.4
  2.9 8.5 %all-to-all-start.1 = ((bf16[16,2,128,128]{3,2,1,0:T(8,128)(2,1)}), bf16[16,2,128,128]{3,2,1,0:T(8,128)(2,1)S(1)}, u32[]{:S(2)}, u32[]{:S(2)}) async-start(bf16[16,2,128,128]{3,2,1,0:T(8,128)(2,1)} %shard_map.87), calls=%async_computation.1 | async-start | bytes 2097152 | tf_op jit(solution)/shard_map/all_to_all | solution.py:279
  11.4 0.0 copy-done.3
  11.4 0.1 collective-permute-start.15
  11.5 0.0 copy-done.4
  11.5 0.5 collective-permute-start.16
  12.0 2.2 %shard_map.85 = (bf16[2,128,128]{2,1,0:T(8,128)(2,1)}, bf16[2,128,128]{2,1,0:T(8,128)(2,1)}, bf16[2,128,128]{2,1,0:T(8,128)(2,1)}, bf16[2,128,128]{2,1,0:T(8,128...) custom-call(bf16[128,4096]{1,0:T(8,128)(2,1)} %bitcast.12, ...), custom_call_target="tpu_custom_call" | custom-call | bytes 2097152 | tf_op jit(solution)/shard_map/pallas_call | solution.py:218
  14.2 2.0 %collective-permute-start = (bf16[2,128,128]{2,1,0:T(8,128)(2,1)}, bf16[2,128,128]{2,1,0:T(8,128)(2,1)S(1)}, u32[]{:S(2)}, u32[]{:S(2)}) collective-permute-start(bf16[2,128,128]{2,1,0:T(8,128)(2,1)} %get-tuple-element.26), channel_id=1, source_target_pairs={{0,1},{1,0},{2,3},{3,2},{4,5},{5,4},{6,7},{7,6},{8,9},{9,8},{10,11... | collective-permute-start | bytes 196616 | tf_op jit(solution)/shard_map/ppermute | solution.py:276
  16.2 1.5 %collective-permute-start.1 = (bf16[2,128,128]{2,1,0:T(8,128)(2,1)}, bf16[2,128,128]{2,1,0:T(8,128)(2,1)S(1)}, u32[]{:S(2)}, u32[]{:S(2)}) collective-permute-start(bf16[2,128,128]{2,1,0:T(8,128)(2,1)} %get-tuple-element.27), channel_id=1, source_target_pairs={{0,2},{1,3},{2,0},{3,1},{4,6},{5,7},{6,4},{7,5},{8,10},{9,11},{10,... | collective-permute-start | bytes 196616 | tf_op jit(solution)/shard_map/ppermute | solution.py:276
  17.7 0.1 collective-permute-start.2
  17.8 1.0 collective-permute-done.refs_3_
  18.8 1.9 %collective-permute-start.3 = (bf16[2,128,128]{2,1,0:T(8,128)(2,1)}, bf16[2,128,128]{2,1,0:T(8,128)(2,1)S(1)}, u32[]{:S(2)}, u32[]{:S(2)}) collective-permute-start(bf16[2,128,128]{2,1,0:T(8,128)(2,1)} %get-tuple-element.29), channel_id=1, source_target_pairs={{0,4},{1,5},{2,6},{3,7},{4,0},{5,1},{6,2},{7,3},{8,12},{9,13},{10,... | collective-permute-start | bytes 196616 | tf_op jit(solution)/shard_map/ppermute | solution.py:276
  20.7 2.4 %collective-permute-done.1.refs_4_ = bf16[2,128,128]{2,1,0:T(8,128)(2,1)S(1)} collective-permute-done((bf16[2,128,128]{2,1,0:T(8,128)(2,1)}, bf16[2,128,128]{2,1,0:T(8,128)(2,1)S(1)}, u32[]{:S(2)}, u32[]{:S(2)}) %collective-permute-start.1) | collective-permute-done | bytes 65568 | tf_op jit(solution)/shard_map/ppermute | solution.py:276
  23.1 1.0 collective-permute-start.4
  24.0 0.3 collective-permute-done.2.refs_5_
  24.3 3.0 %collective-permute-start.5 = (bf16[2,128,128]{2,1,0:T(8,128)(2,1)}, bf16[2,128,128]{2,1,0:T(8,128)(2,1)S(1)}, u32[]{:S(2)}, u32[]{:S(2)}) collective-permute-start(bf16[2,128,128]{2,1,0:T(8,128)(2,1)} %get-tuple-element.31), channel_id=1, source_target_pairs={{0,6},{1,7},{2,4},{3,5},{4,2},{5,3},{6,0},{7,1},{8,14},{9,15},{10,... | collective-permute-start | bytes 196616 | tf_op jit(solution)/shard_map/ppermute | solution.py:276
  27.4 3.7 %collective-permute-done.3.refs_6_ = bf16[2,128,128]{2,1,0:T(8,128)(2,1)S(1)} collective-permute-done((bf16[2,128,128]{2,1,0:T(8,128)(2,1)}, bf16[2,128,128]{2,1,0:T(8,128)(2,1)S(1)}, u32[]{:S(2)}, u32[]{:S(2)}) %collective-permute-start.3) | collective-permute-done | bytes 65568 | tf_op jit(solution)/shard_map/ppermute | solution.py:276
  31.0 4.6 %collective-permute-start.6 = (bf16[2,128,128]{2,1,0:T(8,128)(2,1)}, bf16[2,128,128]{2,1,0:T(8,128)(2,1)S(1)}, u32[]{:S(2)}, u32[]{:S(2)}) collective-permute-start(bf16[2,128,128]{2,1,0:T(8,128)(2,1)} %get-tuple-element.32), channel_id=1, source_target_pairs={{0,7},{1,6},{2,5},{3,4},{4,3},{5,2},{6,1},{7,0},{8,15},{9,14},{10,... | collective-permute-start | bytes 196616 | tf_op jit(solution)/shard_map/ppermute | solution.py:276
  35.7 0.0 collective-permute-done.4.refs_7_
  35.7 1.9 %collective-permute-start.7 = (bf16[2,128,128]{2,1,0:T(8,128)(2,1)}, bf16[2,128,128]{2,1,0:T(8,128)(2,1)S(1)}, u32[]{:S(2)}, u32[]{:S(2)}) collective-permute-start(bf16[2,128,128]{2,1,0:T(8,128)(2,1)} %get-tuple-element.33), channel_id=1, source_target_pairs={{0,8},{1,9},{2,10},{3,11},{4,12},{5,13},{6,14},{7,15},{8,0},{9,1},... | collective-permute-start | bytes 196616 | tf_op jit(solution)/shard_map/ppermute | solution.py:276
  37.6 0.0 collective-permute-done.5.refs_8_
  37.6 3.3 %collective-permute-start.8 = (bf16[2,128,128]{2,1,0:T(8,128)(2,1)}, bf16[2,128,128]{2,1,0:T(8,128)(2,1)S(1)}, u32[]{:S(2)}, u32[]{:S(2)}) collective-permute-start(bf16[2,128,128]{2,1,0:T(8,128)(2,1)} %get-tuple-element.34), channel_id=1, source_target_pairs={{0,9},{1,8},{2,11},{3,10},{4,13},{5,12},{6,15},{7,14},{8,1},{9,0},... | collective-permute-start | bytes 196616 | tf_op jit(solution)/shard_map/ppermute | solution.py:276
  40.8 0.0 collective-permute-done.6.refs_9_
  40.8 3.0 %collective-permute-start.9 = (bf16[2,128,128]{2,1,0:T(8,128)(2,1)}, bf16[2,128,128]{2,1,0:T(8,128)(2,1)S(1)}, u32[]{:S(2)}, u32[]{:S(2)}) collective-permute-start(bf16[2,128,128]{2,1,0:T(8,128)(2,1)} %get-tuple-element.35), channel_id=1, source_target_pairs={{0,10},{1,11},{2,8},{3,9},{4,14},{5,15},{6,12},{7,13},{8,2},{9,3},... | collective-permute-start | bytes 196616 | tf_op jit(solution)/shard_map/ppermute | solution.py:276
  43.8 0.0 collective-permute-done.7.refs_10_
  43.8 0.8 collective-permute-start.10
  44.6 0.0 collective-permute-done.8.refs_11_
  44.6 3.5 %collective-permute-start.11 = (bf16[2,128,128]{2,1,0:T(8,128)(2,1)}, bf16[2,128,128]{2,1,0:T(8,128)(2,1)S(1)}, u32[]{:S(2)}, u32[]{:S(2)}) collective-permute-start(bf16[2,128,128]{2,1,0:T(8,128)(2,1)} %get-tuple-element.37), channel_id=1, source_target_pairs={{0,12},{1,13},{2,14},{3,15},{4,8},{5,9},{6,10},{7,11},{8,4},{9,5},... | collective-permute-start | bytes 196616 | tf_op jit(solution)/shard_map/ppermute | solution.py:276
  48.1 2.0 %collective-permute-done.9.refs_12_ = bf16[2,128,128]{2,1,0:T(8,128)(2,1)S(1)} collective-permute-done((bf16[2,128,128]{2,1,0:T(8,128)(2,1)}, bf16[2,128,128]{2,1,0:T(8,128)(2,1)S(1)}, u32[]{:S(2)}, u32[]{:S(2)}) %collective-permute-start.9) | collective-permute-done | bytes 65568 | tf_op jit(solution)/shard_map/ppermute | solution.py:276
  50.1 2.6 %collective-permute-start.12 = (bf16[2,128,128]{2,1,0:T(8,128)(2,1)}, bf16[2,128,128]{2,1,0:T(8,128)(2,1)S(1)}, u32[]{:S(2)}, u32[]{:S(2)}) collective-permute-start(bf16[2,128,128]{2,1,0:T(8,128)(2,1)} %get-tuple-element.38), channel_id=1, source_target_pairs={{0,13},{1,12},{2,15},{3,14},{4,9},{5,8},{6,11},{7,10},{8,5},{9,4},... | collective-permute-start | bytes 196616 | tf_op jit(solution)/shard_map/ppermute | solution.py:276
  52.7 0.0 collective-permute-done.10.refs_13_
  52.7 2.0 %collective-permute-start.13 = (bf16[2,128,128]{2,1,0:T(8,128)(2,1)}, bf16[2,128,128]{2,1,0:T(8,128)(2,1)S(1)}, u32[]{:S(2)}, u32[]{:S(2)}) collective-permute-start(bf16[2,128,128]{2,1,0:T(8,128)(2,1)} %get-tuple-element.39), channel_id=1, source_target_pairs={{0,14},{1,15},{2,12},{3,13},{4,10},{5,11},{6,8},{7,9},{8,6},{9,7},... | collective-permute-start | bytes 196616 | tf_op jit(solution)/shard_map/ppermute | solution.py:276
  54.8 0.0 collective-permute-done.11.refs_14_
  54.8 3.1 %collective-permute-start.14 = (bf16[2,128,128]{2,1,0:T(8,128)(2,1)}, bf16[2,128,128]{2,1,0:T(8,128)(2,1)S(1)}, u32[]{:S(2)}, u32[]{:S(2)}) collective-permute-start(bf16[2,128,128]{2,1,0:T(8,128)(2,1)} %get-tuple-element.40), channel_id=1, source_target_pairs={{0,15},{1,14},{2,13},{3,12},{4,11},{5,10},{6,9},{7,8},{8,7},{9,6},... | collective-permute-start | bytes 196616 | tf_op jit(solution)/shard_map/ppermute | solution.py:276
  57.8 0.0 collective-permute-done.12.refs_15_
  57.8 2.0 %collective-permute-done.13.refs_16_ = bf16[2,128,128]{2,1,0:T(8,128)(2,1)S(1)} collective-permute-done((bf16[2,128,128]{2,1,0:T(8,128)(2,1)}, bf16[2,128,128]{2,1,0:T(8,128)(2,1)S(1)}, u32[]{:S(2)}, u32[]{:S(2)}) %collective-permute-start.13) | collective-permute-done | bytes 65568 | tf_op jit(solution)/shard_map/ppermute | solution.py:276
  59.9 2.9 %collective-permute-done.14.refs_17_ = bf16[2,128,128]{2,1,0:T(8,128)(2,1)S(1)} collective-permute-done((bf16[2,128,128]{2,1,0:T(8,128)(2,1)}, bf16[2,128,128]{2,1,0:T(8,128)(2,1)S(1)}, u32[]{:S(2)}, u32[]{:S(2)}) %collective-permute-start.14) | collective-permute-done | bytes 65568 | tf_op jit(solution)/shard_map/ppermute | solution.py:276
  62.8 0.0 collective-permute-done.15.refs_19_.refs_4_
  62.8 0.0 collective-permute-done.16.refs_21_.refs_6_
  62.9 0.5 copy-done.22
  63.5 0.0 copy-done.9
  63.5 0.1 copy-done.5
  63.7 0.6 copy-done.6
  64.3 13.2 %shard_map.86 = (bf16[16,128,128]{2,1,0:T(8,128)(2,1)}, bf16[2,1024,128]{2,1,0:T(8,128)(2,1)}, bf16[2,1024,128]{2,1,0:T(8,128)(2,1)}) custom-call(s32[2]{0:T(128)} %refs_0_.3, s32[2]{0:T(128)} %refs_1_.3, bf16[2,128,128]{2,1,0:T(8,128)(2,1)} %get-tuple-element.25.refs_2_, bf16[2,128,128]{2,1,0:T(8,128)(2,1)} %copy-done.8, bf16[2,128,128]{2,1,0:T(8,128)(2,1)} %copy-done.9, ...), custom_call_target="tpu_custom_call" | custom-call | flops 3397386240 | bytes 3670016 | tf_op jit(solution)/shard_map/pallas_call | solution.py:159
  77.4 0.0 all-to-all-done.1.refs_2_
  77.4 0.0 copy-start
  77.5 0.0 copy-start.7
  77.5 4.6 %all-to-all-start = ((bf16[16,128,128]{2,1,0:T(8,128)(2,1)}), bf16[16,128,128]{2,1,0:T(8,128)(2,1)S(1)}, u32[]{:S(2)}, u32[]{:S(2)}) async-start(bf16[16,128,128]{2,1,0:T(8,128)(2,1)} %get-tuple-element.41), calls=%async_computation | async-start | bytes 1048576 | tf_op jit(solution)/shard_map/all_to_all | solution.py:300
  82.1 0.0 copy-done.7
  82.1 0.1 collective-permute-start.17
  82.2 12.9 %shard_map.88 = (bf16[16,128,128]{2,1,0:T(8,128)(2,1)}, bf16[2,1024,128]{2,1,0:T(8,128)(2,1)}, bf16[2,1024,128]{2,1,0:T(8,128)(2,1)}) custom-call(s32[2]{0:T(128)} %refs_0_.3, s32[2]{0:T(128)} %refs_1_.3, bf16[16,2,128,128]{3,2,1,0:T(8,128)(2,1)} %copy-done, bf16[1024,256]{1,0:T(8,128)(2,1)} %refs_3_.1, bf16[1024,256]{1,0:T(8,128)(2,1)} %copy-done.5, ...), custom_call_target="tpu_custom_call" | custom-call | flops 3397386240 | bytes 3670016 | tf_op jit(solution)/shard_map/pallas_call | solution.py:159
  95.1 0.6 collective-permute-start.18
  95.7 0.0 all-to-all-done.refs_0_
  95.7 7.0 %all-to-all-start.2 = ((bf16[16,128,128]{2,1,0:T(8,128)(2,1)}), bf16[16,128,128]{2,1,0:T(8,128)(2,1)S(1)}, u32[]{:S(2)}, u32[]{:S(2)}) async-start(bf16[16,128,128]{2,1,0:T(8,128)(2,1)} %get-tuple-element.42), calls=%async_computation.2 | async-start | bytes 1048576 | tf_op jit(solution)/shard_map/all_to_all | solution.py:300
  102.7 0.0 collective-permute-done.17
  102.7 0.1 add_convert_fusion.1
  102.9 0.0 collective-permute-done.18
  102.9 1.0 copy-done.2
  103.9 0.1 add_convert_fusion
  104.1 1.1 pad_maximum_fusion
  105.2 12.8 %all-to-all-done.2.refs_1_ = bf16[16,128,128]{2,1,0:T(8,128)(2,1)S(1)} async-done(((bf16[16,128,128]{2,1,0:T(8,128)(2,1)}), bf16[16,128,128]{2,1,0:T(8,128)(2,1)S(1)}, u32[]{:S(2)}, u32[]{:S(2)}) %all-to-all-start.2) | async-done | bytes 524320 | tf_op jit(solution)/shard_map/all_to_all | solution.py:300
  118.0 1.6 %unpack.1 = bf16[128,4096]{1,0:T(8,128)(2,1)} custom-call(bf16[16,128,128]{2,1,0:T(8,128)(2,1)S(1)} %all-to-all-done.refs_0_, bf16[16,128,128]{2,1,0:T(8,128)(2,1)S(1)} %all-to-all-done.2.refs_1_), custom_call_target="tpu_custom_call" | custom-call | tf_op jit(solution)/shard_map/unpack/pallas_call | solution.py:252
  (36 shorter events, 0.1 us)
Async XLA Ops:
  2.9 8.5 %copy-start.3 = (bf16[1024,256]{1,0:T(8,128)(2,1)S(1)}, bf16[1024,256]{1,0:T(8,128)(2,1)}, u32[]{:S(2)}) copy-start(bf16[1024,256]{1,0:T(8,128)(2,1)} %refs_3_.1) | copy-start | bytes 1572868
  2.9 8.6 %copy-start.4 = (bf16[1024,256]{1,0:T(8,128)(2,1)S(1)}, bf16[1024,256]{1,0:T(8,128)(2,1)}, u32[]{:S(2)}) copy-start(bf16[1024,256]{1,0:T(8,128)(2,1)} %refs_5_.1) | copy-start | bytes 1572868
  2.9 74.5 %all-to-all-start.1 = ((bf16[16,2,128,128]{3,2,1,0:T(8,128)(2,1)}), bf16[16,2,128,128]{3,2,1,0:T(8,128)(2,1)S(1)}, u32[]{:S(2)}, u32[]{:S(2)}) async-start(bf16[16,2,128,128]{3,2,1,0:T(8,128)(2,1)} %shard_map.87), calls=%async_computation.1 | async-start | bytes 2097152 | tf_op jit(solution)/shard_map/all_to_all | solution.py:279
  11.4 51.4 %collective-permute-start.15 = (bf16[1024,256]{1,0:T(8,128)(2,1)S(1)}, bf16[1024,256]{1,0:T(8,128)(2,1)S(1)}, u32[]{:S(2)}, u32[]{:S(2)}) collective-permute-start(bf16[1024,256]{1,0:T(8,128)(2,1)S(1)} %copy-done.3), channel_id=1, source_target_pairs={{0,16},{16,0},{1,17},{17,1},{2,18},{18,2},{3,19},{19,3},{4,20},{20... | collective-permute-start | bytes 1572872 | tf_op jit(solution)/shard_map/ppermute | solution.py:285
  11.5 51.3 %collective-permute-start.16 = (bf16[1024,256]{1,0:T(8,128)(2,1)S(1)}, bf16[1024,256]{1,0:T(8,128)(2,1)S(1)}, u32[]{:S(2)}, u32[]{:S(2)}) collective-permute-start(bf16[1024,256]{1,0:T(8,128)(2,1)S(1)} %copy-done.4), channel_id=1, source_target_pairs={{0,16},{16,0},{1,17},{17,1},{2,18},{18,2},{3,19},{19,3},{4,20},{20... | collective-permute-start | bytes 1572872 | tf_op jit(solution)/shard_map/ppermute | solution.py:286
  14.2 4.5 %collective-permute-start = (bf16[2,128,128]{2,1,0:T(8,128)(2,1)}, bf16[2,128,128]{2,1,0:T(8,128)(2,1)S(1)}, u32[]{:S(2)}, u32[]{:S(2)}) collective-permute-start(bf16[2,128,128]{2,1,0:T(8,128)(2,1)} %get-tuple-element.26), channel_id=1, source_target_pairs={{0,1},{1,0},{2,3},{3,2},{4,5},{5,4},{6,7},{7,6},{8,9},{9,8},{10,11... | collective-permute-start | bytes 196616 | tf_op jit(solution)/shard_map/ppermute | solution.py:276
  16.2 6.8 %collective-permute-start.1 = (bf16[2,128,128]{2,1,0:T(8,128)(2,1)}, bf16[2,128,128]{2,1,0:T(8,128)(2,1)S(1)}, u32[]{:S(2)}, u32[]{:S(2)}) collective-permute-start(bf16[2,128,128]{2,1,0:T(8,128)(2,1)} %get-tuple-element.27), channel_id=1, source_target_pairs={{0,2},{1,3},{2,0},{3,1},{4,6},{5,7},{6,4},{7,5},{8,10},{9,11},{10,... | collective-permute-start | bytes 196616 | tf_op jit(solution)/shard_map/ppermute | solution.py:276
  17.7 6.7 %collective-permute-start.2 = (bf16[2,128,128]{2,1,0:T(8,128)(2,1)}, bf16[2,128,128]{2,1,0:T(8,128)(2,1)S(1)}, u32[]{:S(2)}, u32[]{:S(2)}) collective-permute-start(bf16[2,128,128]{2,1,0:T(8,128)(2,1)} %get-tuple-element.28), channel_id=1, source_target_pairs={{0,3},{1,2},{2,1},{3,0},{4,7},{5,6},{6,5},{7,4},{8,11},{9,10},{10,... | collective-permute-start | bytes 196616 | tf_op jit(solution)/shard_map/ppermute | solution.py:276
  18.8 44.7 %copy-start.8 = (bf16[2,128,128]{2,1,0:T(8,128)(2,1)}, bf16[2,128,128]{2,1,0:T(8,128)(2,1)S(1)}, u32[]{:S(2)}) copy-start(bf16[2,128,128]{2,1,0:T(8,128)(2,1)S(1)} %collective-permute-done.refs_3_) | copy-start | bytes 196612
  18.8 12.3 %collective-permute-start.3 = (bf16[2,128,128]{2,1,0:T(8,128)(2,1)}, bf16[2,128,128]{2,1,0:T(8,128)(2,1)S(1)}, u32[]{:S(2)}, u32[]{:S(2)}) collective-permute-start(bf16[2,128,128]{2,1,0:T(8,128)(2,1)} %get-tuple-element.29), channel_id=1, source_target_pairs={{0,4},{1,5},{2,6},{3,7},{4,0},{5,1},{6,2},{7,3},{8,12},{9,13},{10,... | collective-permute-start | bytes 196616 | tf_op jit(solution)/shard_map/ppermute | solution.py:276
  23.1 40.4 %copy-start.9 = (bf16[2,128,128]{2,1,0:T(8,128)(2,1)}, bf16[2,128,128]{2,1,0:T(8,128)(2,1)S(1)}, u32[]{:S(2)}) copy-start(bf16[2,128,128]{2,1,0:T(8,128)(2,1)S(1)} %collective-permute-done.1.refs_4_) | copy-start | bytes 196612
  23.1 12.6 %collective-permute-start.4 = (bf16[2,128,128]{2,1,0:T(8,128)(2,1)}, bf16[2,128,128]{2,1,0:T(8,128)(2,1)S(1)}, u32[]{:S(2)}, u32[]{:S(2)}) collective-permute-start(bf16[2,128,128]{2,1,0:T(8,128)(2,1)} %get-tuple-element.30), channel_id=1, source_target_pairs={{0,5},{1,4},{2,7},{3,6},{4,1},{5,0},{6,3},{7,2},{8,13},{9,12},{10,... | collective-permute-start | bytes 196616 | tf_op jit(solution)/shard_map/ppermute | solution.py:276
  24.3 39.1 %copy-start.10 = (bf16[2,128,128]{2,1,0:T(8,128)(2,1)}, bf16[2,128,128]{2,1,0:T(8,128)(2,1)S(1)}, u32[]{:S(2)}) copy-start(bf16[2,128,128]{2,1,0:T(8,128)(2,1)S(1)} %collective-permute-done.2.refs_5_) | copy-start | bytes 196612
  24.3 13.2 %collective-permute-start.5 = (bf16[2,128,128]{2,1,0:T(8,128)(2,1)}, bf16[2,128,128]{2,1,0:T(8,128)(2,1)S(1)}, u32[]{:S(2)}, u32[]{:S(2)}) collective-permute-start(bf16[2,128,128]{2,1,0:T(8,128)(2,1)} %get-tuple-element.31), channel_id=1, source_target_pairs={{0,6},{1,7},{2,4},{3,5},{4,2},{5,3},{6,0},{7,1},{8,14},{9,15},{10,... | collective-permute-start | bytes 196616 | tf_op jit(solution)/shard_map/ppermute | solution.py:276
  31.0 32.4 %copy-start.11 = (bf16[2,128,128]{2,1,0:T(8,128)(2,1)}, bf16[2,128,128]{2,1,0:T(8,128)(2,1)S(1)}, u32[]{:S(2)}) copy-start(bf16[2,128,128]{2,1,0:T(8,128)(2,1)S(1)} %collective-permute-done.3.refs_6_) | copy-start | bytes 196612
  31.0 9.8 %collective-permute-start.6 = (bf16[2,128,128]{2,1,0:T(8,128)(2,1)}, bf16[2,128,128]{2,1,0:T(8,128)(2,1)S(1)}, u32[]{:S(2)}, u32[]{:S(2)}) collective-permute-start(bf16[2,128,128]{2,1,0:T(8,128)(2,1)} %get-tuple-element.32), channel_id=1, source_target_pairs={{0,7},{1,6},{2,5},{3,4},{4,3},{5,2},{6,1},{7,0},{8,15},{9,14},{10,... | collective-permute-start | bytes 196616 | tf_op jit(solution)/shard_map/ppermute | solution.py:276
  35.7 27.8 %copy-start.12 = (bf16[2,128,128]{2,1,0:T(8,128)(2,1)}, bf16[2,128,128]{2,1,0:T(8,128)(2,1)S(1)}, u32[]{:S(2)}) copy-start(bf16[2,128,128]{2,1,0:T(8,128)(2,1)S(1)} %collective-permute-done.4.refs_7_) | copy-start | bytes 196612
  35.7 8.2 %collective-permute-start.7 = (bf16[2,128,128]{2,1,0:T(8,128)(2,1)}, bf16[2,128,128]{2,1,0:T(8,128)(2,1)S(1)}, u32[]{:S(2)}, u32[]{:S(2)}) collective-permute-start(bf16[2,128,128]{2,1,0:T(8,128)(2,1)} %get-tuple-element.33), channel_id=1, source_target_pairs={{0,8},{1,9},{2,10},{3,11},{4,12},{5,13},{6,14},{7,15},{8,0},{9,1},... | collective-permute-start | bytes 196616 | tf_op jit(solution)/shard_map/ppermute | solution.py:276
  37.6 25.9 %copy-start.13 = (bf16[2,128,128]{2,1,0:T(8,128)(2,1)}, bf16[2,128,128]{2,1,0:T(8,128)(2,1)S(1)}, u32[]{:S(2)}) copy-start(bf16[2,128,128]{2,1,0:T(8,128)(2,1)S(1)} %collective-permute-done.5.refs_8_) | copy-start | bytes 196612
  37.6 7.1 %collective-permute-start.8 = (bf16[2,128,128]{2,1,0:T(8,128)(2,1)}, bf16[2,128,128]{2,1,0:T(8,128)(2,1)S(1)}, u32[]{:S(2)}, u32[]{:S(2)}) collective-permute-start(bf16[2,128,128]{2,1,0:T(8,128)(2,1)} %get-tuple-element.34), channel_id=1, source_target_pairs={{0,9},{1,8},{2,11},{3,10},{4,13},{5,12},{6,15},{7,14},{8,1},{9,0},... | collective-permute-start | bytes 196616 | tf_op jit(solution)/shard_map/ppermute | solution.py:276
  40.8 22.0 %copy-start.14 = (bf16[2,128,128]{2,1,0:T(8,128)(2,1)}, bf16[2,128,128]{2,1,0:T(8,128)(2,1)S(1)}, u32[]{:S(2)}) copy-start(bf16[2,128,128]{2,1,0:T(8,128)(2,1)S(1)} %collective-permute-done.6.refs_9_) | copy-start | bytes 196612
  40.8 9.3 %collective-permute-start.9 = (bf16[2,128,128]{2,1,0:T(8,128)(2,1)}, bf16[2,128,128]{2,1,0:T(8,128)(2,1)S(1)}, u32[]{:S(2)}, u32[]{:S(2)}) collective-permute-start(bf16[2,128,128]{2,1,0:T(8,128)(2,1)} %get-tuple-element.35), channel_id=1, source_target_pairs={{0,10},{1,11},{2,8},{3,9},{4,14},{5,15},{6,12},{7,13},{8,2},{9,3},... | collective-permute-start | bytes 196616 | tf_op jit(solution)/shard_map/ppermute | solution.py:276
  43.8 19.0 %copy-start.15 = (bf16[2,128,128]{2,1,0:T(8,128)(2,1)}, bf16[2,128,128]{2,1,0:T(8,128)(2,1)S(1)}, u32[]{:S(2)}) copy-start(bf16[2,128,128]{2,1,0:T(8,128)(2,1)S(1)} %collective-permute-done.7.refs_10_) | copy-start | bytes 196612
  43.8 8.9 %collective-permute-start.10 = (bf16[2,128,128]{2,1,0:T(8,128)(2,1)}, bf16[2,128,128]{2,1,0:T(8,128)(2,1)S(1)}, u32[]{:S(2)}, u32[]{:S(2)}) collective-permute-start(bf16[2,128,128]{2,1,0:T(8,128)(2,1)} %get-tuple-element.36), channel_id=1, source_target_pairs={{0,11},{1,10},{2,9},{3,8},{4,15},{5,14},{6,13},{7,12},{8,3},{9,2},... | collective-permute-start | bytes 196616 | tf_op jit(solution)/shard_map/ppermute | solution.py:276
  44.6 18.3 %copy-start.16 = (bf16[2,128,128]{2,1,0:T(8,128)(2,1)}, bf16[2,128,128]{2,1,0:T(8,128)(2,1)S(1)}, u32[]{:S(2)}) copy-start(bf16[2,128,128]{2,1,0:T(8,128)(2,1)S(1)} %collective-permute-done.8.refs_11_) | copy-start | bytes 196612
  44.6 10.1 %collective-permute-start.11 = (bf16[2,128,128]{2,1,0:T(8,128)(2,1)}, bf16[2,128,128]{2,1,0:T(8,128)(2,1)S(1)}, u32[]{:S(2)}, u32[]{:S(2)}) collective-permute-start(bf16[2,128,128]{2,1,0:T(8,128)(2,1)} %get-tuple-element.37), channel_id=1, source_target_pairs={{0,12},{1,13},{2,14},{3,15},{4,8},{5,9},{6,10},{7,11},{8,4},{9,5},... | collective-permute-start | bytes 196616 | tf_op jit(solution)/shard_map/ppermute | solution.py:276
  50.1 12.8 %copy-start.17 = (bf16[2,128,128]{2,1,0:T(8,128)(2,1)}, bf16[2,128,128]{2,1,0:T(8,128)(2,1)S(1)}, u32[]{:S(2)}) copy-start(bf16[2,128,128]{2,1,0:T(8,128)(2,1)S(1)} %collective-permute-done.9.refs_12_) | copy-start | bytes 196612
  50.1 7.7 %collective-permute-start.12 = (bf16[2,128,128]{2,1,0:T(8,128)(2,1)}, bf16[2,128,128]{2,1,0:T(8,128)(2,1)S(1)}, u32[]{:S(2)}, u32[]{:S(2)}) collective-permute-start(bf16[2,128,128]{2,1,0:T(8,128)(2,1)} %get-tuple-element.38), channel_id=1, source_target_pairs={{0,13},{1,12},{2,15},{3,14},{4,9},{5,8},{6,11},{7,10},{8,5},{9,4},... | collective-permute-start | bytes 196616 | tf_op jit(solution)/shard_map/ppermute | solution.py:276
  52.7 10.2 %copy-start.18 = (bf16[2,128,128]{2,1,0:T(8,128)(2,1)}, bf16[2,128,128]{2,1,0:T(8,128)(2,1)S(1)}, u32[]{:S(2)}) copy-start(bf16[2,128,128]{2,1,0:T(8,128)(2,1)S(1)} %collective-permute-done.10.refs_13_) | copy-start | bytes 196612
  52.7 7.2 %collective-permute-start.13 = (bf16[2,128,128]{2,1,0:T(8,128)(2,1)}, bf16[2,128,128]{2,1,0:T(8,128)(2,1)S(1)}, u32[]{:S(2)}, u32[]{:S(2)}) collective-permute-start(bf16[2,128,128]{2,1,0:T(8,128)(2,1)} %get-tuple-element.39), channel_id=1, source_target_pairs={{0,14},{1,15},{2,12},{3,13},{4,10},{5,11},{6,8},{7,9},{8,6},{9,7},... | collective-permute-start | bytes 196616 | tf_op jit(solution)/shard_map/ppermute | solution.py:276
  54.8 8.1 %copy-start.19 = (bf16[2,128,128]{2,1,0:T(8,128)(2,1)}, bf16[2,128,128]{2,1,0:T(8,128)(2,1)S(1)}, u32[]{:S(2)}) copy-start(bf16[2,128,128]{2,1,0:T(8,128)(2,1)S(1)} %collective-permute-done.11.refs_14_) | copy-start | bytes 196612
  54.8 8.1 %collective-permute-start.14 = (bf16[2,128,128]{2,1,0:T(8,128)(2,1)}, bf16[2,128,128]{2,1,0:T(8,128)(2,1)S(1)}, u32[]{:S(2)}, u32[]{:S(2)}) collective-permute-start(bf16[2,128,128]{2,1,0:T(8,128)(2,1)} %get-tuple-element.40), channel_id=1, source_target_pairs={{0,15},{1,14},{2,13},{3,12},{4,11},{5,10},{6,9},{7,8},{8,7},{9,6},... | collective-permute-start | bytes 196616 | tf_op jit(solution)/shard_map/ppermute | solution.py:276
  57.8 5.1 %copy-start.20 = (bf16[2,128,128]{2,1,0:T(8,128)(2,1)}, bf16[2,128,128]{2,1,0:T(8,128)(2,1)S(1)}, u32[]{:S(2)}) copy-start(bf16[2,128,128]{2,1,0:T(8,128)(2,1)S(1)} %collective-permute-done.12.refs_15_) | copy-start | bytes 196612
  59.9 3.0 %copy-start.21 = (bf16[2,128,128]{2,1,0:T(8,128)(2,1)}, bf16[2,128,128]{2,1,0:T(8,128)(2,1)S(1)}, u32[]{:S(2)}) copy-start(bf16[2,128,128]{2,1,0:T(8,128)(2,1)S(1)} %collective-permute-done.13.refs_16_) | copy-start | bytes 196612
  62.8 0.6 copy-start.22
  62.8 0.8 copy-start.5
  63.5 0.8 copy-start.6
  77.4 4.7 %copy-start = (bf16[16,2,128,128]{3,2,1,0:T(8,128)(2,1)}, bf16[16,2,128,128]{3,2,1,0:T(8,128)(2,1)S(1)}, u32[]{:S(2)}) copy-start(bf16[16,2,128,128]{3,2,1,0:T(8,128)(2,1)S(1)} %all-to-all-done.1.refs_2_) | copy-start | bytes 3145732
  77.5 4.6 %copy-start.7 = (bf16[2,1024,128]{2,1,0:T(8,128)(2,1)S(1)}, bf16[2,1024,128]{2,1,0:T(8,128)(2,1)}, u32[]{:S(2)}) copy-start(bf16[2,1024,128]{2,1,0:T(8,128)(2,1)} %get-tuple-element.44) | copy-start | bytes 1572868
  77.5 18.2 %all-to-all-start = ((bf16[16,128,128]{2,1,0:T(8,128)(2,1)}), bf16[16,128,128]{2,1,0:T(8,128)(2,1)S(1)}, u32[]{:S(2)}, u32[]{:S(2)}) async-start(bf16[16,128,128]{2,1,0:T(8,128)(2,1)} %get-tuple-element.41), calls=%async_computation | async-start | bytes 1048576 | tf_op jit(solution)/shard_map/all_to_all | solution.py:300
  82.1 20.6 %collective-permute-start.17 = (bf16[2,1024,128]{2,1,0:T(8,128)(2,1)S(1)}, bf16[2,1024,128]{2,1,0:T(8,128)(2,1)S(1)}, u32[]{:S(2)}, u32[]{:S(2)}) collective-permute-start(bf16[2,1024,128]{2,1,0:T(8,128)(2,1)S(1)} %copy-done.7), channel_id=1, source_target_pairs={{0,16},{16,0},{1,17},{17,1},{2,18},{18,2},{3,19},{19,3},{4,20},{20... | collective-permute-start | bytes 1572872 | tf_op jit(solution)/shard_map/ppermute | solution.py:293
  95.1 7.8 %collective-permute-start.18 = (bf16[2,1024,128]{2,1,0:T(8,128)(2,1)}, bf16[2,1024,128]{2,1,0:T(8,128)(2,1)S(1)}, u32[]{:S(2)}, u32[]{:S(2)}) collective-permute-start(bf16[2,1024,128]{2,1,0:T(8,128)(2,1)} %get-tuple-element.46), channel_id=1, source_target_pairs={{0,16},{16,0},{1,17},{17,1},{2,18},{18,2},{3,19},{19,3},{4,20},{20... | collective-permute-start | bytes 1572872 | tf_op jit(solution)/shard_map/ppermute | solution.py:293
  95.7 7.1 %copy-start.1 = (bf16[2,1024,128]{2,1,0:T(8,128)(2,1)S(1)}, bf16[2,1024,128]{2,1,0:T(8,128)(2,1)}, u32[]{:S(2)}) copy-start(bf16[2,1024,128]{2,1,0:T(8,128)(2,1)} %get-tuple-element.43) | copy-start | bytes 1572868
  95.7 22.3 %all-to-all-start.2 = ((bf16[16,128,128]{2,1,0:T(8,128)(2,1)}), bf16[16,128,128]{2,1,0:T(8,128)(2,1)S(1)}, u32[]{:S(2)}, u32[]{:S(2)}) async-start(bf16[16,128,128]{2,1,0:T(8,128)(2,1)} %get-tuple-element.42), calls=%async_computation.2 | async-start | bytes 1048576 | tf_op jit(solution)/shard_map/all_to_all | solution.py:300
  102.9 1.0 copy-start.2
where the time goes:
time: 121 us; the launch traced here: 120 us
  starting transfers between devices  55.6 us (46%)
  Pallas kernels  32.2 us (27%)
  waiting for transfers between devices  27.1 us (22%)
  local copies, waits for them, and re-layouts  2.42 us (2%)
  other arithmetic  1.36 us (1%)
    ppermute x15, starting transfers between devices, received(): lax.ppermute(sent[k], 'seq', [(i, i ^ k) for i in range(parts)])  34.2 us
    pallas_call x2, Pallas kernels, attention_backward(): pl.pallas_call(functools.partial(backward_kernel, block, past, n_blocks,...  26.1 us
    ppermute x15, waiting for transfers between devices, received(): lax.ppermute(sent[k], 'seq', [(i, i ^ k) for i in range(parts)])  14.3 us
    all_to_all x2, waiting for transfers between devices, on_device(): lax.all_to_all(dq, 'seq', split_axis=0, concat_axis=0, tiled=True)  12.8 us
    all_to_all x2, starting transfers between devices, on_device(): lax.all_to_all(dq, 'seq', split_axis=0, concat_axis=0, tiled=True)  11.6 us
    all_to_all x1, starting transfers between devices, received(): lax.all_to_all(sent, 'seq', split_axis=0, concat_axis=0, tiled=True)  8.48 us
    pallas_call x2, Pallas kernels, pack(): pl.pallas_call(kernel, in_specs=[pl.BlockSpec(memory_space=pl.ANY)] * 2,...  4.48 us
  transfers between devices with their start and end apart: 22, of which 8 were waited for; matrix products, arithmetic and copies ran while one was open for 1% of the time, Pallas kernels for 24%

commit v1 on v0

--- a/solution.py
+++ b/solution.py
@@ -23,6 +23,10 @@
 
 def nn_dot(a, b):
     return lax.dot_general(a, b, (((1,), (0,)), ((), ())), preferred_element_type=jnp.float32)
+
+
+def aligned(value, size):
+    return value if isinstance(value, int) else pl.multiple_of(value, size)
 
 
 def backward_kernel(block, past, n_blocks, head, n_pieces, n_parts, *refs):
@@ -34,7 +38,6 @@
     sums, refs = refs[:n_parts], refs[n_parts:]
     held_ref, k_ref, v_ref, kt_ref, bias_ref, p_ref, gp_ref, dk_acc, dv_acc, sems = refs
 
-    number = pl.program_id(0)
     depth_id, seq_id = lax.axis_index("depth"), lax.axis_index("seq")
     shift = offsets_ref[depth_id]
     span = windows_ref[depth_id]
@@ -45,49 +48,46 @@
     def part_at(n):
         return pl.ds(pl.multiple_of((depth_id ^ n) * part_rows, part_rows) if n_parts > 1 else 0, part_rows)
 
-    @pl.when(number == 0)
-    def _():
-        columns = pl.ds(head * HEAD_DIM, HEAD_DIM)
-        copies = []
-        for n in range(n_parts):
-            for parts, ref in ((key_parts, k_ref), (value_parts, v_ref)):
-                copies.append((parts[n].at[:, columns], ref.at[part_at(n)]))
-        for k in range(n_pieces):
-            copies.append((pieces[k], held_ref.at[seq_id ^ k] if n_pieces > 1 else held_ref))
-        copies = [
-            pltpu.make_async_copy(source, target, sems.at[n])
-            for n, (source, target) in enumerate(copies)
-        ]
-        for copy in copies:
-            copy.start()
-        dk_acc[...] = jnp.zeros_like(dk_acc)
-        dv_acc[...] = jnp.zeros_like(dv_acc)
-        ahead = lax.broadcasted_iota(jnp.int32, (8, block), 0) - lax.broadcasted_iota(
-            jnp.int32, (8, block), 1
-        )
-        for back in range(past + 1):
-            for row in range(0, block, 8):
-                lead = row - back * block
-                keep = ahead > shift - span - lead
-                if lead + 7 > 0:
-                    keep = keep & (ahead <= shift - lead)
-                bias_ref[back, pl.ds(row, 8), :] = jnp.where(keep, 0.0, -jnp.inf)
-        for copy in copies:
-            copy.wait()
-        kt_ref[...] = k_ref[...].T
-
-    def step(n_past):
-        first_row = pl.multiple_of(number * block, block)
+    columns = pl.ds(head * HEAD_DIM, HEAD_DIM)
+    copies = [(part.at[:, columns], k_ref.at[part_at(n)]) for n, part in enumerate(key_parts)]
+    copies += [(part.at[:, columns], v_ref.at[part_at(n)]) for n, part in enumerate(value_parts)]
+    for k in range(n_pieces):
+        copies.append((pieces[k], held_ref.at[seq_id ^ k] if n_pieces > 1 else held_ref))
+    copies = [
+        pltpu.make_async_copy(source, target, sems.at[n]) for n, (source, target) in enumerate(copies)
+    ]
+    for copy in copies:
+        copy.start()
+    dk_acc[...] = jnp.zeros_like(dk_acc)
+    dv_acc[...] = jnp.zeros_like(dv_acc)
+    ahead = lax.broadcasted_iota(jnp.int32, (8, block), 0) - lax.broadcasted_iota(
+        jnp.int32, (8, block), 1
+    )
+    for back in range(past + 1):
+        for row in range(0, block, 8):
+            lead = row - back * block
+            keep = ahead > shift - span - lead
+            if lead + 7 > 0:
+                keep = keep & (ahead <= shift - lead)
+            bias_ref[back, pl.ds(row, 8), :] = jnp.where(keep, 0.0, -jnp.inf)
+    for copy in copies[:n_parts]:
+        copy.wait()
+    kt_ref[...] = k_ref[...].T
+    for copy in copies[n_parts:]:
+        copy.wait()
+
+    def step(number, n_past):
+        first_row = aligned(number * block, block)
         per_block = block // tok_rows
         held = pl.ds(number * per_block, per_block)
         query = held_ref[held, 0].reshape(block, HEAD_DIM)
         grad = held_ref[held, 1].reshape(block, HEAD_DIM)
-        edge_first = pl.multiple_of(jnp.minimum(first_row + block, seq_total - EDGE), EDGE)
+        edge_first = aligned(jnp.minimum(first_row + block, seq_total - EDGE), EDGE)
         edge_key = edge_first + lax.broadcasted_iota(jnp.int32, (EDGE, block), 0)
         edge_query = first_row + lax.broadcasted_iota(jnp.int32, (EDGE, block), 1)
         edge_in = (edge_key >= first_row + block) & (edge_key - edge_query <= shift)
         tiles = [
-            (pl.multiple_of((number - back) * block, block), block, back * block, back)
+            (aligned((number - back) * block, block), block, back * block, back)
             for back in range(n_past + 1)
         ]
         tiles.append((edge_first, EDGE, (past + 1) * block, None))
@@ -130,17 +130,20 @@
                 )
             else:
                 dq_t = dq_t + nn_dot(kt_ref[:, here], grad_score)
-        dq_ref[...] = (dq_t * SCALING).T.astype(jnp.bfloat16).reshape(dq_ref.shape)
-
-    for n_past in range(past):
-        pl.when(number == n_past)(functools.partial(step, n_past))
-    pl.when(number >= past)(functools.partial(step, past))
-
-    @pl.when(number == n_blocks - 1)
-    def _():
-        for n in range(n_parts):
-            sums[n][0] = (dk_acc[part_at(n), :] * SCALING).astype(jnp.bfloat16)
-            sums[n][1] = dv_acc[part_at(n), :].astype(jnp.bfloat16)
+        dq_ref[held] = (
+            (dq_t * SCALING).T.astype(jnp.bfloat16).reshape(per_block, tok_rows, HEAD_DIM)
+        )
+
+    for number in range(past):
+        step(number, number)
+
+    @pl.loop(past, n_blocks)
+    def _(number):
+        step(number, past)
+
+    for n in range(n_parts):
+        sums[n][0] = (dk_acc[part_at(n), :] * SCALING).astype(jnp.bfloat16)
+        sums[n][1] = dv_acc[part_at(n), :].astype(jnp.bfloat16)
 
 
 def attention_backward(offsets, windows, pieces, key_parts, value_parts, head):
@@ -149,7 +152,6 @@
     seq_total = key_parts[0].shape[0] * n_parts
     sources = seq_total // tok_rows
     block = min(2 * tok_rows, seq_total)
-    per_block = block // tok_rows
     n_blocks = seq_total // block
     past = min(-(-WIN // block), n_blocks - 1)
     rows = (past + 1) * block + EDGE
@@ -158,25 +160,21 @@
     sums_shape = (2, seq_total // n_parts, HEAD_DIM)
     dq, *sums = pl.pallas_call(
         functools.partial(backward_kernel, block, past, n_blocks, head, n_pieces, n_parts),
-        grid_spec=pltpu.PrefetchScalarGridSpec(
-            num_scalar_prefetch=2,
-            grid=(n_blocks,),
-            in_specs=[pl.BlockSpec(memory_space=pl.ANY)] * (n_pieces + 2 * n_parts),
-            out_specs=[pl.BlockSpec((per_block, tok_rows, HEAD_DIM), lambda i, *_: (i, 0, 0))]
-            + [pl.BlockSpec(sums_shape, lambda i, *_: (0, 0, 0))] * n_parts,
-            scratch_shapes=[
-                pltpu.VMEM((sources, 2, tok_rows, HEAD_DIM), bf16),
-                pltpu.VMEM((seq_total, HEAD_DIM), bf16),
-                pltpu.VMEM((seq_total, HEAD_DIM), bf16),
-                pltpu.VMEM((HEAD_DIM, seq_total), bf16),
-                pltpu.VMEM((past + 1, block, block), f32),
-                pltpu.VMEM((rows, block), f32),
-                pltpu.VMEM((rows, block), f32),
-                pltpu.VMEM((seq_total, HEAD_DIM), f32),
-                pltpu.VMEM((seq_total, HEAD_DIM), f32),
-                pltpu.SemaphoreType.DMA((n_pieces + 2 * n_parts,)),
-            ],
-        ),
+        in_specs=[pl.BlockSpec(memory_space=pltpu.SMEM)] * 2
+        + [pl.BlockSpec(memory_space=pl.ANY)] * (n_pieces + 2 * n_parts),
+        out_specs=[pl.BlockSpec(memory_space=pltpu.VMEM)] * (1 + n_parts),
+        scratch_shapes=[
+            pltpu.VMEM((sources, 2, tok_rows, HEAD_DIM), bf16),
+            pltpu.VMEM((seq_total, HEAD_DIM), bf16),
+            pltpu.VMEM((seq_total, HEAD_DIM), bf16),
+            pltpu.VMEM((HEAD_DIM, seq_total), bf16),
+            pltpu.VMEM((past + 1, block, block), f32),
+            pltpu.VMEM((rows, block), f32),
+            pltpu.VMEM((rows, block), f32),
+            pltpu.VMEM((seq_total, HEAD_DIM), f32),
+            pltpu.VMEM((seq_total, HEAD_DIM), f32),
+            pltpu.SemaphoreType.DMA((n_pieces + 2 * n_parts,)),
+        ],
         out_shape=[jax.ShapeDtypeStruct((sources, tok_rows, HEAD_DIM), bf16)]
         + [jax.ShapeDtypeStruct(sums_shape, bf16)] * n_parts,
         cost_estimate=pl.CostEstimate(
@@ -269,7 +267,7 @@
     grad_out = grad_out.reshape(tok_rows, model_width)
 
     def received(head):
-        if head + 1 < heads and parts & (parts - 1) == 0:
+        if head > 0 and parts & (parts - 1) == 0:
             sent = pack(head, heads, queries, grad_out, parts)
             landed = [sent[0]]
             for k in range(1, parts):

time: 121 us -> 118 us (0.975)
  Pallas kernels: 32.2 us -> 30.1 us
    pallas_call x2, Pallas kernels: 26.1 us -> 24 us  [attention_backward(): pl.pallas_call(functools.partial(backward_kernel, block, past, n_blocks,...]
  transfers between devices with their start and end apart: 22 -> 22, of which waited for: 8 -> 8; matrix products, arithmetic and copies ran while one was open for 1% -> 1% of each run, Pallas kernels for 24% -> 22%
where the time goes in v1:
time: 118 us
  starting transfers between devices  55.5 us (47%)
  Pallas kernels  30.1 us (26%)
  waiting for transfers between devices  27.2 us (23%)
  local copies, waits for them, and re-layouts  2.42 us (2%)
  other arithmetic  1.36 us (1%)
    ppermute x15, starting transfers between devices, received(): lax.ppermute(sent[k], 'seq', [(i, i ^ k) for i in range(parts)])  34.2 us
    pallas_call x2, Pallas kernels, attention_backward(): pl.pallas_call(functools.partial(backward_kernel, block, past, n_blocks,...  24 us
    ppermute x15, waiting for transfers between devices, received(): lax.ppermute(sent[k], 'seq', [(i, i ^ k) for i in range(parts)])  14.4 us
    all_to_all x2, waiting for transfers between devices, on_device(): lax.all_to_all(dq, 'seq', split_axis=0, concat_axis=0, tiled=True)  12.8 us
    all_to_all x2, starting transfers between devices, on_device(): lax.all_to_all(dq, 'seq', split_axis=0, concat_axis=0, tiled=True)  11.6 us
    all_to_all x1, starting transfers between devices, received(): lax.all_to_all(sent, 'seq', split_axis=0, concat_axis=0, tiled=True)  8.48 us
    pallas_call x2, Pallas kernels, pack(): pl.pallas_call(kernel, in_specs=[pl.BlockSpec(memory_space=pl.ANY)] * 2,...  4.48 us
  transfers between devices with their start and end apart: 22, of which 8 were waited for; matrix products, arithmetic and copies ran while one was open for 1% of the time, Pallas kernels for 22%

profile of v1, /device:TPU:0, one launch (start us, length us, event | category | flops | bytes accessed | tf_op | source)
XLA Modules:
  0.0 117.7 jit_solution(11392569986907660118)
XLA Ops:
  0.6 2.2 %shard_map.85 = bf16[16,2,128,128]{3,2,1,0:T(8,128)(2,1)} custom-call(bf16[128,4096]{1,0:T(8,128)(2,1)} %bitcast.11, bf16[128,4096]{1,0:T(8,128)(2,1)} %bitcast.13), custom_call_target="tpu_custom_call" | custom-call | bytes 2097152 | tf_op jit(solution)/shard_map/pallas_call | solution.py:216
  2.9 0.0 copy-start.3
  2.9 0.0 copy-start.4
  2.9 8.5 %all-to-all-start = ((bf16[16,2,128,128]{3,2,1,0:T(8,128)(2,1)}), bf16[16,2,128,128]{3,2,1,0:T(8,128)(2,1)S(1)}, u32[]{:S(2)}, u32[]{:S(2)}) async-start(bf16[16,2,128,128]{3,2,1,0:T(8,128)(2,1)} %shard_map.85), calls=%async_computation | async-start | bytes 2097152 | tf_op jit(solution)/shard_map/all_to_all | solution.py:277
  11.4 0.1 collective-permute-start
  11.5 0.0 copy-done.4
  11.5 0.5 collective-permute-start.1
  12.0 2.2 %shard_map.87 = (bf16[2,128,128]{2,1,0:T(8,128)(2,1)}, bf16[2,128,128]{2,1,0:T(8,128)(2,1)}, bf16[2,128,128]{2,1,0:T(8,128)(2,1)}, bf16[2,128,128]{2,1,0:T(8,128...) custom-call(bf16[128,4096]{1,0:T(8,128)(2,1)} %bitcast.12, ...), custom_call_target="tpu_custom_call" | custom-call | bytes 2097152 | tf_op jit(solution)/shard_map/pallas_call | solution.py:216
  14.2 2.0 %collective-permute-start.2 = (bf16[2,128,128]{2,1,0:T(8,128)(2,1)}, bf16[2,128,128]{2,1,0:T(8,128)(2,1)S(1)}, u32[]{:S(2)}, u32[]{:S(2)}) collective-permute-start(bf16[2,128,128]{2,1,0:T(8,128)(2,1)} %get-tuple-element.27), channel_id=1, source_target_pairs={{0,1},{1,0},{2,3},{3,2},{4,5},{5,4},{6,7},{7,6},{8,9},{9,8},{10,11... | collective-permute-start | bytes 196616 | tf_op jit(solution)/shard_map/ppermute | solution.py:274
  16.2 1.5 %collective-permute-start.3 = (bf16[2,128,128]{2,1,0:T(8,128)(2,1)}, bf16[2,128,128]{2,1,0:T(8,128)(2,1)S(1)}, u32[]{:S(2)}, u32[]{:S(2)}) collective-permute-start(bf16[2,128,128]{2,1,0:T(8,128)(2,1)} %get-tuple-element.28), channel_id=1, source_target_pairs={{0,2},{1,3},{2,0},{3,1},{4,6},{5,7},{6,4},{7,5},{8,10},{9,11},{10,... | collective-permute-start | bytes 196616 | tf_op jit(solution)/shard_map/ppermute | solution.py:274
  17.7 0.1 collective-permute-start.4
  17.8 1.0 collective-permute-done.2.refs_3_
  18.8 1.9 %collective-permute-start.5 = (bf16[2,128,128]{2,1,0:T(8,128)(2,1)}, bf16[2,128,128]{2,1,0:T(8,128)(2,1)S(1)}, u32[]{:S(2)}, u32[]{:S(2)}) collective-permute-start(bf16[2,128,128]{2,1,0:T(8,128)(2,1)} %get-tuple-element.30), channel_id=1, source_target_pairs={{0,4},{1,5},{2,6},{3,7},{4,0},{5,1},{6,2},{7,3},{8,12},{9,13},{10,... | collective-permute-start | bytes 196616 | tf_op jit(solution)/shard_map/ppermute | solution.py:274
  20.7 2.4 %collective-permute-done.3.refs_4_ = bf16[2,128,128]{2,1,0:T(8,128)(2,1)S(1)} collective-permute-done((bf16[2,128,128]{2,1,0:T(8,128)(2,1)}, bf16[2,128,128]{2,1,0:T(8,128)(2,1)S(1)}, u32[]{:S(2)}, u32[]{:S(2)}) %collective-permute-start.3) | collective-permute-done | bytes 65568 | tf_op jit(solution)/shard_map/ppermute | solution.py:274
  23.1 1.0 collective-permute-start.6
  24.0 0.3 collective-permute-done.4.refs_5_
  24.4 3.0 %collective-permute-start.7 = (bf16[2,128,128]{2,1,0:T(8,128)(2,1)}, bf16[2,128,128]{2,1,0:T(8,128)(2,1)S(1)}, u32[]{:S(2)}, u32[]{:S(2)}) collective-permute-start(bf16[2,128,128]{2,1,0:T(8,128)(2,1)} %get-tuple-element.32), channel_id=1, source_target_pairs={{0,6},{1,7},{2,4},{3,5},{4,2},{5,3},{6,0},{7,1},{8,14},{9,15},{10,... | collective-permute-start | bytes 196616 | tf_op jit(solution)/shard_map/ppermute | solution.py:274
  27.4 3.7 %collective-permute-done.5.refs_6_ = bf16[2,128,128]{2,1,0:T(8,128)(2,1)S(1)} collective-permute-done((bf16[2,128,128]{2,1,0:T(8,128)(2,1)}, bf16[2,128,128]{2,1,0:T(8,128)(2,1)S(1)}, u32[]{:S(2)}, u32[]{:S(2)}) %collective-permute-start.5) | collective-permute-done | bytes 65568 | tf_op jit(solution)/shard_map/ppermute | solution.py:274
  31.0 4.6 %collective-permute-start.8 = (bf16[2,128,128]{2,1,0:T(8,128)(2,1)}, bf16[2,128,128]{2,1,0:T(8,128)(2,1)S(1)}, u32[]{:S(2)}, u32[]{:S(2)}) collective-permute-start(bf16[2,128,128]{2,1,0:T(8,128)(2,1)} %get-tuple-element.33), channel_id=1, source_target_pairs={{0,7},{1,6},{2,5},{3,4},{4,3},{5,2},{6,1},{7,0},{8,15},{9,14},{10,... | collective-permute-start | bytes 196616 | tf_op jit(solution)/shard_map/ppermute | solution.py:274
  35.7 0.0 collective-permute-done.6.refs_7_
  35.7 1.9 %collective-permute-start.9 = (bf16[2,128,128]{2,1,0:T(8,128)(2,1)}, bf16[2,128,128]{2,1,0:T(8,128)(2,1)S(1)}, u32[]{:S(2)}, u32[]{:S(2)}) collective-permute-start(bf16[2,128,128]{2,1,0:T(8,128)(2,1)} %get-tuple-element.34), channel_id=1, source_target_pairs={{0,8},{1,9},{2,10},{3,11},{4,12},{5,13},{6,14},{7,15},{8,0},{9,1},... | collective-permute-start | bytes 196616 | tf_op jit(solution)/shard_map/ppermute | solution.py:274
  37.6 0.0 collective-permute-done.7.refs_8_
  37.6 3.3 %collective-permute-start.10 = (bf16[2,128,128]{2,1,0:T(8,128)(2,1)}, bf16[2,128,128]{2,1,0:T(8,128)(2,1)S(1)}, u32[]{:S(2)}, u32[]{:S(2)}) collective-permute-start(bf16[2,128,128]{2,1,0:T(8,128)(2,1)} %get-tuple-element.35), channel_id=1, source_target_pairs={{0,9},{1,8},{2,11},{3,10},{4,13},{5,12},{6,15},{7,14},{8,1},{9,0},... | collective-permute-start | bytes 196616 | tf_op jit(solution)/shard_map/ppermute | solution.py:274
  40.8 0.0 collective-permute-done.8.refs_9_
  40.8 3.0 %collective-permute-start.11 = (bf16[2,128,128]{2,1,0:T(8,128)(2,1)}, bf16[2,128,128]{2,1,0:T(8,128)(2,1)S(1)}, u32[]{:S(2)}, u32[]{:S(2)}) collective-permute-start(bf16[2,128,128]{2,1,0:T(8,128)(2,1)} %get-tuple-element.36), channel_id=1, source_target_pairs={{0,10},{1,11},{2,8},{3,9},{4,14},{5,15},{6,12},{7,13},{8,2},{9,3},... | collective-permute-start | bytes 196616 | tf_op jit(solution)/shard_map/ppermute | solution.py:274
  43.8 0.0 collective-permute-done.9.refs_10_
  43.8 0.8 collective-permute-start.12
  44.6 0.0 collective-permute-done.10.refs_11_
  44.6 3.5 %collective-permute-start.13 = (bf16[2,128,128]{2,1,0:T(8,128)(2,1)}, bf16[2,128,128]{2,1,0:T(8,128)(2,1)S(1)}, u32[]{:S(2)}, u32[]{:S(2)}) collective-permute-start(bf16[2,128,128]{2,1,0:T(8,128)(2,1)} %get-tuple-element.38), channel_id=1, source_target_pairs={{0,12},{1,13},{2,14},{3,15},{4,8},{5,9},{6,10},{7,11},{8,4},{9,5},... | collective-permute-start | bytes 196616 | tf_op jit(solution)/shard_map/ppermute | solution.py:274
  48.1 2.0 %collective-permute-done.11.refs_12_ = bf16[2,128,128]{2,1,0:T(8,128)(2,1)S(1)} collective-permute-done((bf16[2,128,128]{2,1,0:T(8,128)(2,1)}, bf16[2,128,128]{2,1,0:T(8,128)(2,1)S(1)}, u32[]{:S(2)}, u32[]{:S(2)}) %collective-permute-start.11) | collective-permute-done | bytes 65568 | tf_op jit(solution)/shard_map/ppermute | solution.py:274
  50.1 2.6 %collective-permute-start.14 = (bf16[2,128,128]{2,1,0:T(8,128)(2,1)}, bf16[2,128,128]{2,1,0:T(8,128)(2,1)S(1)}, u32[]{:S(2)}, u32[]{:S(2)}) collective-permute-start(bf16[2,128,128]{2,1,0:T(8,128)(2,1)} %get-tuple-element.39), channel_id=1, source_target_pairs={{0,13},{1,12},{2,15},{3,14},{4,9},{5,8},{6,11},{7,10},{8,5},{9,4},... | collective-permute-start | bytes 196616 | tf_op jit(solution)/shard_map/ppermute | solution.py:274
  52.7 0.0 collective-permute-done.12.refs_13_
  52.7 2.0 %collective-permute-start.15 = (bf16[2,128,128]{2,1,0:T(8,128)(2,1)}, bf16[2,128,128]{2,1,0:T(8,128)(2,1)S(1)}, u32[]{:S(2)}, u32[]{:S(2)}) collective-permute-start(bf16[2,128,128]{2,1,0:T(8,128)(2,1)} %get-tuple-element.40), channel_id=1, source_target_pairs={{0,14},{1,15},{2,12},{3,13},{4,10},{5,11},{6,8},{7,9},{8,6},{9,7},... | collective-permute-start | bytes 196616 | tf_op jit(solution)/shard_map/ppermute | solution.py:274
  54.8 0.0 collective-permute-done.13.refs_14_
  54.8 3.1 %collective-permute-start.16 = (bf16[2,128,128]{2,1,0:T(8,128)(2,1)}, bf16[2,128,128]{2,1,0:T(8,128)(2,1)S(1)}, u32[]{:S(2)}, u32[]{:S(2)}) collective-permute-start(bf16[2,128,128]{2,1,0:T(8,128)(2,1)} %get-tuple-element.41), channel_id=1, source_target_pairs={{0,15},{1,14},{2,13},{3,12},{4,11},{5,10},{6,9},{7,8},{8,7},{9,6},... | collective-permute-start | bytes 196616 | tf_op jit(solution)/shard_map/ppermute | solution.py:274
  57.8 0.0 collective-permute-done.14.refs_15_
  57.8 2.0 %collective-permute-done.15.refs_16_ = bf16[2,128,128]{2,1,0:T(8,128)(2,1)S(1)} collective-permute-done((bf16[2,128,128]{2,1,0:T(8,128)(2,1)}, bf16[2,128,128]{2,1,0:T(8,128)(2,1)S(1)}, u32[]{:S(2)}, u32[]{:S(2)}) %collective-permute-start.15) | collective-permute-done | bytes 65568 | tf_op jit(solution)/shard_map/ppermute | solution.py:274
  59.9 2.9 %collective-permute-done.16.refs_17_ = bf16[2,128,128]{2,1,0:T(8,128)(2,1)S(1)} collective-permute-done((bf16[2,128,128]{2,1,0:T(8,128)(2,1)}, bf16[2,128,128]{2,1,0:T(8,128)(2,1)S(1)}, u32[]{:S(2)}, u32[]{:S(2)}) %collective-permute-start.16) | collective-permute-done | bytes 65568 | tf_op jit(solution)/shard_map/ppermute | solution.py:274
  62.8 0.0 collective-permute-done.refs_4_.refs_19_
  62.8 0.0 collective-permute-done.1.refs_6_.refs_21_
  62.9 0.5 copy-done.22
  63.5 0.0 copy-done.10
  63.5 0.0 copy-done.11
  63.5 0.0 copy-done.12
  63.5 0.0 copy-done.13
  63.5 0.1 copy-done.5
  63.7 0.6 copy-done.6
  64.3 12.0 %shard_map.88 = (bf16[16,128,128]{2,1,0:T(8,128)(2,1)}, bf16[2,1024,128]{2,1,0:T(8,128)(2,1)}, bf16[2,1024,128]{2,1,0:T(8,128)(2,1)}) custom-call(s32[2]{0:T(128)} %refs_0_.3, s32[2]{0:T(128)} %refs_1_.3, bf16[2,128,128]{2,1,0:T(8,128)(2,1)} %get-tuple-element.26.refs_2_, bf16[2,128,128]{2,1,0:T(8,128)(2,1)} %copy-done.8, bf16[2,128,128]{2,1,0:T(8,128)(2,1)} %copy-done.9, ...), custom_call_target="tpu_custom_call" | custom-call | flops 3397386240 | bytes 3670016 | tf_op jit(solution)/shard_map/pallas_call | solution.py:161
  76.3 0.0 all-to-all-done.refs_2_
  76.3 0.0 copy-start
  76.3 4.6 %all-to-all-start.2 = ((bf16[16,128,128]{2,1,0:T(8,128)(2,1)}), bf16[16,128,128]{2,1,0:T(8,128)(2,1)S(1)}, u32[]{:S(2)}, u32[]{:S(2)}) async-start(bf16[16,128,128]{2,1,0:T(8,128)(2,1)} %get-tuple-element.42), calls=%async_computation.2 | async-start | bytes 1048576 | tf_op jit(solution)/shard_map/all_to_all | solution.py:298
  81.0 0.1 collective-permute-start.18
  81.0 12.0 %shard_map.86 = (bf16[16,128,128]{2,1,0:T(8,128)(2,1)}, bf16[2,1024,128]{2,1,0:T(8,128)(2,1)}, bf16[2,1024,128]{2,1,0:T(8,128)(2,1)}) custom-call(s32[2]{0:T(128)} %refs_0_.3, s32[2]{0:T(128)} %refs_1_.3, bf16[16,2,128,128]{3,2,1,0:T(8,128)(2,1)} %copy-done, bf16[1024,256]{1,0:T(8,128)(2,1)} %refs_18_.1, bf16[1024,256]{1,0:T(8,128)(2,1)} %copy-done.5, ...), custom_call_target="tpu_custom_call" | custom-call | flops 3397386240 | bytes 3670016 | tf_op jit(solution)/shard_map/pallas_call | solution.py:161
  93.1 0.6 collective-permute-start.17
  93.6 0.0 all-to-all-done.2.refs_1_
  93.6 7.0 %all-to-all-start.1 = ((bf16[16,128,128]{2,1,0:T(8,128)(2,1)}), bf16[16,128,128]{2,1,0:T(8,128)(2,1)S(1)}, u32[]{:S(2)}, u32[]{:S(2)}) async-start(bf16[16,128,128]{2,1,0:T(8,128)(2,1)} %get-tuple-element.25), calls=%async_computation.1 | async-start | bytes 1048576 | tf_op jit(solution)/shard_map/all_to_all | solution.py:298
  100.7 0.0 collective-permute-done.18
  100.7 0.1 add_convert_fusion
  100.9 0.0 collective-permute-done.17
  100.9 1.0 copy-done.2
  101.9 0.1 add_convert_fusion.1
  102.1 1.1 pad_maximum_fusion
  103.1 12.8 %all-to-all-done.1.refs_0_ = bf16[16,128,128]{2,1,0:T(8,128)(2,1)S(1)} async-done(((bf16[16,128,128]{2,1,0:T(8,128)(2,1)}), bf16[16,128,128]{2,1,0:T(8,128)(2,1)S(1)}, u32[]{:S(2)}, u32[]{:S(2)}) %all-to-all-start.1) | async-done | bytes 524320 | tf_op jit(solution)/shard_map/all_to_all | solution.py:298
  115.9 1.6 %unpack.1 = bf16[128,4096]{1,0:T(8,128)(2,1)} custom-call(bf16[16,128,128]{2,1,0:T(8,128)(2,1)S(1)} %all-to-all-done.1.refs_0_, bf16[16,128,128]{2,1,0:T(8,128)(2,1)S(1)} %all-to-all-done.2.refs_1_), custom_call_target="tpu_custom_call" | custom-call | tf_op jit(solution)/shard_map/unpack/pallas_call | solution.py:250
  (36 shorter events, 0.1 us)
Async XLA Ops:
  2.9 8.5 %copy-start.3 = (bf16[1024,256]{1,0:T(8,128)(2,1)S(1)}, bf16[1024,256]{1,0:T(8,128)(2,1)}, u32[]{:S(2)}) copy-start(bf16[1024,256]{1,0:T(8,128)(2,1)} %refs_18_.1) | copy-start | bytes 1572868
  2.9 8.6 %copy-start.4 = (bf16[1024,256]{1,0:T(8,128)(2,1)S(1)}, bf16[1024,256]{1,0:T(8,128)(2,1)}, u32[]{:S(2)}) copy-start(bf16[1024,256]{1,0:T(8,128)(2,1)} %refs_20_.1) | copy-start | bytes 1572868
  2.9 73.4 %all-to-all-start = ((bf16[16,2,128,128]{3,2,1,0:T(8,128)(2,1)}), bf16[16,2,128,128]{3,2,1,0:T(8,128)(2,1)S(1)}, u32[]{:S(2)}, u32[]{:S(2)}) async-start(bf16[16,2,128,128]{3,2,1,0:T(8,128)(2,1)} %shard_map.85), calls=%async_computation | async-start | bytes 2097152 | tf_op jit(solution)/shard_map/all_to_all | solution.py:277
  11.4 51.4 %collective-permute-start = (bf16[1024,256]{1,0:T(8,128)(2,1)S(1)}, bf16[1024,256]{1,0:T(8,128)(2,1)S(1)}, u32[]{:S(2)}, u32[]{:S(2)}) collective-permute-start(bf16[1024,256]{1,0:T(8,128)(2,1)S(1)} %copy-done.3), channel_id=1, source_target_pairs={{0,16},{16,0},{1,17},{17,1},{2,18},{18,2},{3,19},{19,3},{4,20},{20... | collective-permute-start | bytes 1572872 | tf_op jit(solution)/shard_map/ppermute | solution.py:283
  11.5 51.3 %collective-permute-start.1 = (bf16[1024,256]{1,0:T(8,128)(2,1)S(1)}, bf16[1024,256]{1,0:T(8,128)(2,1)S(1)}, u32[]{:S(2)}, u32[]{:S(2)}) collective-permute-start(bf16[1024,256]{1,0:T(8,128)(2,1)S(1)} %copy-done.4), channel_id=1, source_target_pairs={{0,16},{16,0},{1,17},{17,1},{2,18},{18,2},{3,19},{19,3},{4,20},{20... | collective-permute-start | bytes 1572872 | tf_op jit(solution)/shard_map/ppermute | solution.py:284
  14.2 4.5 %collective-permute-start.2 = (bf16[2,128,128]{2,1,0:T(8,128)(2,1)}, bf16[2,128,128]{2,1,0:T(8,128)(2,1)S(1)}, u32[]{:S(2)}, u32[]{:S(2)}) collective-permute-start(bf16[2,128,128]{2,1,0:T(8,128)(2,1)} %get-tuple-element.27), channel_id=1, source_target_pairs={{0,1},{1,0},{2,3},{3,2},{4,5},{5,4},{6,7},{7,6},{8,9},{9,8},{10,11... | collective-permute-start | bytes 196616 | tf_op jit(solution)/shard_map/ppermute | solution.py:274
  16.2 6.9 %collective-permute-start.3 = (bf16[2,128,128]{2,1,0:T(8,128)(2,1)}, bf16[2,128,128]{2,1,0:T(8,128)(2,1)S(1)}, u32[]{:S(2)}, u32[]{:S(2)}) collective-permute-start(bf16[2,128,128]{2,1,0:T(8,128)(2,1)} %get-tuple-element.28), channel_id=1, source_target_pairs={{0,2},{1,3},{2,0},{3,1},{4,6},{5,7},{6,4},{7,5},{8,10},{9,11},{10,... | collective-permute-start | bytes 196616 | tf_op jit(solution)/shard_map/ppermute | solution.py:274
  17.7 6.7 %collective-permute-start.4 = (bf16[2,128,128]{2,1,0:T(8,128)(2,1)}, bf16[2,128,128]{2,1,0:T(8,128)(2,1)S(1)}, u32[]{:S(2)}, u32[]{:S(2)}) collective-permute-start(bf16[2,128,128]{2,1,0:T(8,128)(2,1)} %get-tuple-element.29), channel_id=1, source_target_pairs={{0,3},{1,2},{2,1},{3,0},{4,7},{5,6},{6,5},{7,4},{8,11},{9,10},{10,... | collective-permute-start | bytes 196616 | tf_op jit(solution)/shard_map/ppermute | solution.py:274
  18.8 44.7 %copy-start.8 = (bf16[2,128,128]{2,1,0:T(8,128)(2,1)}, bf16[2,128,128]{2,1,0:T(8,128)(2,1)S(1)}, u32[]{:S(2)}) copy-start(bf16[2,128,128]{2,1,0:T(8,128)(2,1)S(1)} %collective-permute-done.2.refs_3_) | copy-start | bytes 196612
  18.8 12.3 %collective-permute-start.5 = (bf16[2,128,128]{2,1,0:T(8,128)(2,1)}, bf16[2,128,128]{2,1,0:T(8,128)(2,1)S(1)}, u32[]{:S(2)}, u32[]{:S(2)}) collective-permute-start(bf16[2,128,128]{2,1,0:T(8,128)(2,1)} %get-tuple-element.30), channel_id=1, source_target_pairs={{0,4},{1,5},{2,6},{3,7},{4,0},{5,1},{6,2},{7,3},{8,12},{9,13},{10,... | collective-permute-start | bytes 196616 | tf_op jit(solution)/shard_map/ppermute | solution.py:274
  23.1 40.4 %copy-start.9 = (bf16[2,128,128]{2,1,0:T(8,128)(2,1)}, bf16[2,128,128]{2,1,0:T(8,128)(2,1)S(1)}, u32[]{:S(2)}) copy-start(bf16[2,128,128]{2,1,0:T(8,128)(2,1)S(1)} %collective-permute-done.3.refs_4_) | copy-start | bytes 196612
  23.1 12.6 %collective-permute-start.6 = (bf16[2,128,128]{2,1,0:T(8,128)(2,1)}, bf16[2,128,128]{2,1,0:T(8,128)(2,1)S(1)}, u32[]{:S(2)}, u32[]{:S(2)}) collective-permute-start(bf16[2,128,128]{2,1,0:T(8,128)(2,1)} %get-tuple-element.31), channel_id=1, source_target_pairs={{0,5},{1,4},{2,7},{3,6},{4,1},{5,0},{6,3},{7,2},{8,13},{9,12},{10,... | collective-permute-start | bytes 196616 | tf_op jit(solution)/shard_map/ppermute | solution.py:274
  24.4 39.1 %copy-start.10 = (bf16[2,128,128]{2,1,0:T(8,128)(2,1)}, bf16[2,128,128]{2,1,0:T(8,128)(2,1)S(1)}, u32[]{:S(2)}) copy-start(bf16[2,128,128]{2,1,0:T(8,128)(2,1)S(1)} %collective-permute-done.4.refs_5_) | copy-start | bytes 196612
  24.4 13.2 %collective-permute-start.7 = (bf16[2,128,128]{2,1,0:T(8,128)(2,1)}, bf16[2,128,128]{2,1,0:T(8,128)(2,1)S(1)}, u32[]{:S(2)}, u32[]{:S(2)}) collective-permute-start(bf16[2,128,128]{2,1,0:T(8,128)(2,1)} %get-tuple-element.32), channel_id=1, source_target_pairs={{0,6},{1,7},{2,4},{3,5},{4,2},{5,3},{6,0},{7,1},{8,14},{9,15},{10,... | collective-permute-start | bytes 196616 | tf_op jit(solution)/shard_map/ppermute | solution.py:274
  31.0 32.4 %copy-start.11 = (bf16[2,128,128]{2,1,0:T(8,128)(2,1)}, bf16[2,128,128]{2,1,0:T(8,128)(2,1)S(1)}, u32[]{:S(2)}) copy-start(bf16[2,128,128]{2,1,0:T(8,128)(2,1)S(1)} %collective-permute-done.5.refs_6_) | copy-start | bytes 196612
  31.0 9.8 %collective-permute-start.8 = (bf16[2,128,128]{2,1,0:T(8,128)(2,1)}, bf16[2,128,128]{2,1,0:T(8,128)(2,1)S(1)}, u32[]{:S(2)}, u32[]{:S(2)}) collective-permute-start(bf16[2,128,128]{2,1,0:T(8,128)(2,1)} %get-tuple-element.33), channel_id=1, source_target_pairs={{0,7},{1,6},{2,5},{3,4},{4,3},{5,2},{6,1},{7,0},{8,15},{9,14},{10,... | collective-permute-start | bytes 196616 | tf_op jit(solution)/shard_map/ppermute | solution.py:274
  35.7 27.8 %copy-start.12 = (bf16[2,128,128]{2,1,0:T(8,128)(2,1)}, bf16[2,128,128]{2,1,0:T(8,128)(2,1)S(1)}, u32[]{:S(2)}) copy-start(bf16[2,128,128]{2,1,0:T(8,128)(2,1)S(1)} %collective-permute-done.6.refs_7_) | copy-start | bytes 196612
  35.7 8.2 %collective-permute-start.9 = (bf16[2,128,128]{2,1,0:T(8,128)(2,1)}, bf16[2,128,128]{2,1,0:T(8,128)(2,1)S(1)}, u32[]{:S(2)}, u32[]{:S(2)}) collective-permute-start(bf16[2,128,128]{2,1,0:T(8,128)(2,1)} %get-tuple-element.34), channel_id=1, source_target_pairs={{0,8},{1,9},{2,10},{3,11},{4,12},{5,13},{6,14},{7,15},{8,0},{9,1},... | collective-permute-start | bytes 196616 | tf_op jit(solution)/shard_map/ppermute | solution.py:274
  37.6 25.9 %copy-start.13 = (bf16[2,128,128]{2,1,0:T(8,128)(2,1)}, bf16[2,128,128]{2,1,0:T(8,128)(2,1)S(1)}, u32[]{:S(2)}) copy-start(bf16[2,128,128]{2,1,0:T(8,128)(2,1)S(1)} %collective-permute-done.7.refs_8_) | copy-start | bytes 196612
  37.6 7.1 %collective-permute-start.10 = (bf16[2,128,128]{2,1,0:T(8,128)(2,1)}, bf16[2,128,128]{2,1,0:T(8,128)(2,1)S(1)}, u32[]{:S(2)}, u32[]{:S(2)}) collective-permute-start(bf16[2,128,128]{2,1,0:T(8,128)(2,1)} %get-tuple-element.35), channel_id=1, source_target_pairs={{0,9},{1,8},{2,11},{3,10},{4,13},{5,12},{6,15},{7,14},{8,1},{9,0},... | collective-permute-start | bytes 196616 | tf_op jit(solution)/shard_map/ppermute | solution.py:274
  40.8 22.0 %copy-start.14 = (bf16[2,128,128]{2,1,0:T(8,128)(2,1)}, bf16[2,128,128]{2,1,0:T(8,128)(2,1)S(1)}, u32[]{:S(2)}) copy-start(bf16[2,128,128]{2,1,0:T(8,128)(2,1)S(1)} %collective-permute-done.8.refs_9_) | copy-start | bytes 196612
  40.8 9.3 %collective-permute-start.11 = (bf16[2,128,128]{2,1,0:T(8,128)(2,1)}, bf16[2,128,128]{2,1,0:T(8,128)(2,1)S(1)}, u32[]{:S(2)}, u32[]{:S(2)}) collective-permute-start(bf16[2,128,128]{2,1,0:T(8,128)(2,1)} %get-tuple-element.36), channel_id=1, source_target_pairs={{0,10},{1,11},{2,8},{3,9},{4,14},{5,15},{6,12},{7,13},{8,2},{9,3},... | collective-permute-start | bytes 196616 | tf_op jit(solution)/shard_map/ppermute | solution.py:274
  43.8 19.0 %copy-start.15 = (bf16[2,128,128]{2,1,0:T(8,128)(2,1)}, bf16[2,128,128]{2,1,0:T(8,128)(2,1)S(1)}, u32[]{:S(2)}) copy-start(bf16[2,128,128]{2,1,0:T(8,128)(2,1)S(1)} %collective-permute-done.9.refs_10_) | copy-start | bytes 196612
  43.8 8.9 %collective-permute-start.12 = (bf16[2,128,128]{2,1,0:T(8,128)(2,1)}, bf16[2,128,128]{2,1,0:T(8,128)(2,1)S(1)}, u32[]{:S(2)}, u32[]{:S(2)}) collective-permute-start(bf16[2,128,128]{2,1,0:T(8,128)(2,1)} %get-tuple-element.37), channel_id=1, source_target_pairs={{0,11},{1,10},{2,9},{3,8},{4,15},{5,14},{6,13},{7,12},{8,3},{9,2},... | collective-permute-start | bytes 196616 | tf_op jit(solution)/shard_map/ppermute | solution.py:274
  44.6 18.3 %copy-start.16 = (bf16[2,128,128]{2,1,0:T(8,128)(2,1)}, bf16[2,128,128]{2,1,0:T(8,128)(2,1)S(1)}, u32[]{:S(2)}) copy-start(bf16[2,128,128]{2,1,0:T(8,128)(2,1)S(1)} %collective-permute-done.10.refs_11_) | copy-start | bytes 196612
  44.6 10.1 %collective-permute-start.13 = (bf16[2,128,128]{2,1,0:T(8,128)(2,1)}, bf16[2,128,128]{2,1,0:T(8,128)(2,1)S(1)}, u32[]{:S(2)}, u32[]{:S(2)}) collective-permute-start(bf16[2,128,128]{2,1,0:T(8,128)(2,1)} %get-tuple-element.38), channel_id=1, source_target_pairs={{0,12},{1,13},{2,14},{3,15},{4,8},{5,9},{6,10},{7,11},{8,4},{9,5},... | collective-permute-start | bytes 196616 | tf_op jit(solution)/shard_map/ppermute | solution.py:274
  50.1 12.8 %copy-start.17 = (bf16[2,128,128]{2,1,0:T(8,128)(2,1)}, bf16[2,128,128]{2,1,0:T(8,128)(2,1)S(1)}, u32[]{:S(2)}) copy-start(bf16[2,128,128]{2,1,0:T(8,128)(2,1)S(1)} %collective-permute-done.11.refs_12_) | copy-start | bytes 196612
  50.1 7.7 %collective-permute-start.14 = (bf16[2,128,128]{2,1,0:T(8,128)(2,1)}, bf16[2,128,128]{2,1,0:T(8,128)(2,1)S(1)}, u32[]{:S(2)}, u32[]{:S(2)}) collective-permute-start(bf16[2,128,128]{2,1,0:T(8,128)(2,1)} %get-tuple-element.39), channel_id=1, source_target_pairs={{0,13},{1,12},{2,15},{3,14},{4,9},{5,8},{6,11},{7,10},{8,5},{9,4},... | collective-permute-start | bytes 196616 | tf_op jit(solution)/shard_map/ppermute | solution.py:274
  52.7 10.2 %copy-start.18 = (bf16[2,128,128]{2,1,0:T(8,128)(2,1)}, bf16[2,128,128]{2,1,0:T(8,128)(2,1)S(1)}, u32[]{:S(2)}) copy-start(bf16[2,128,128]{2,1,0:T(8,128)(2,1)S(1)} %collective-permute-done.12.refs_13_) | copy-start | bytes 196612
  52.7 7.2 %collective-permute-start.15 = (bf16[2,128,128]{2,1,0:T(8,128)(2,1)}, bf16[2,128,128]{2,1,0:T(8,128)(2,1)S(1)}, u32[]{:S(2)}, u32[]{:S(2)}) collective-permute-start(bf16[2,128,128]{2,1,0:T(8,128)(2,1)} %get-tuple-element.40), channel_id=1, source_target_pairs={{0,14},{1,15},{2,12},{3,13},{4,10},{5,11},{6,8},{7,9},{8,6},{9,7},... | collective-permute-start | bytes 196616 | tf_op jit(solution)/shard_map/ppermute | solution.py:274
  54.8 8.1 %copy-start.19 = (bf16[2,128,128]{2,1,0:T(8,128)(2,1)}, bf16[2,128,128]{2,1,0:T(8,128)(2,1)S(1)}, u32[]{:S(2)}) copy-start(bf16[2,128,128]{2,1,0:T(8,128)(2,1)S(1)} %collective-permute-done.13.refs_14_) | copy-start | bytes 196612
  54.8 8.1 %collective-permute-start.16 = (bf16[2,128,128]{2,1,0:T(8,128)(2,1)}, bf16[2,128,128]{2,1,0:T(8,128)(2,1)S(1)}, u32[]{:S(2)}, u32[]{:S(2)}) collective-permute-start(bf16[2,128,128]{2,1,0:T(8,128)(2,1)} %get-tuple-element.41), channel_id=1, source_target_pairs={{0,15},{1,14},{2,13},{3,12},{4,11},{5,10},{6,9},{7,8},{8,7},{9,6},... | collective-permute-start | bytes 196616 | tf_op jit(solution)/shard_map/ppermute | solution.py:274
  57.8 5.1 %copy-start.20 = (bf16[2,128,128]{2,1,0:T(8,128)(2,1)}, bf16[2,128,128]{2,1,0:T(8,128)(2,1)S(1)}, u32[]{:S(2)}) copy-start(bf16[2,128,128]{2,1,0:T(8,128)(2,1)S(1)} %collective-permute-done.14.refs_15_) | copy-start | bytes 196612
  59.9 3.0 %copy-start.21 = (bf16[2,128,128]{2,1,0:T(8,128)(2,1)}, bf16[2,128,128]{2,1,0:T(8,128)(2,1)S(1)}, u32[]{:S(2)}) copy-start(bf16[2,128,128]{2,1,0:T(8,128)(2,1)S(1)} %collective-permute-done.15.refs_16_) | copy-start | bytes 196612
  62.8 0.6 copy-start.22
  62.8 0.8 copy-start.5
  63.5 0.8 copy-start.6
  76.3 4.7 %copy-start = (bf16[16,2,128,128]{3,2,1,0:T(8,128)(2,1)}, bf16[16,2,128,128]{3,2,1,0:T(8,128)(2,1)S(1)}, u32[]{:S(2)}) copy-start(bf16[16,2,128,128]{3,2,1,0:T(8,128)(2,1)S(1)} %all-to-all-done.refs_2_) | copy-start | bytes 3145732
  76.3 4.6 %copy-start.7 = (bf16[2,1024,128]{2,1,0:T(8,128)(2,1)S(1)}, bf16[2,1024,128]{2,1,0:T(8,128)(2,1)}, u32[]{:S(2)}) copy-start(bf16[2,1024,128]{2,1,0:T(8,128)(2,1)} %get-tuple-element.46) | copy-start | bytes 1572868
  76.3 17.3 %all-to-all-start.2 = ((bf16[16,128,128]{2,1,0:T(8,128)(2,1)}), bf16[16,128,128]{2,1,0:T(8,128)(2,1)S(1)}, u32[]{:S(2)}, u32[]{:S(2)}) async-start(bf16[16,128,128]{2,1,0:T(8,128)(2,1)} %get-tuple-element.42), calls=%async_computation.2 | async-start | bytes 1048576 | tf_op jit(solution)/shard_map/all_to_all | solution.py:298
  81.0 19.7 %collective-permute-start.18 = (bf16[2,1024,128]{2,1,0:T(8,128)(2,1)S(1)}, bf16[2,1024,128]{2,1,0:T(8,128)(2,1)S(1)}, u32[]{:S(2)}, u32[]{:S(2)}) collective-permute-start(bf16[2,1024,128]{2,1,0:T(8,128)(2,1)S(1)} %copy-done.7), channel_id=1, source_target_pairs={{0,16},{16,0},{1,17},{17,1},{2,18},{18,2},{3,19},{19,3},{4,20},{20... | collective-permute-start | bytes 1572872 | tf_op jit(solution)/shard_map/ppermute | solution.py:291
  93.1 7.8 %collective-permute-start.17 = (bf16[2,1024,128]{2,1,0:T(8,128)(2,1)}, bf16[2,1024,128]{2,1,0:T(8,128)(2,1)S(1)}, u32[]{:S(2)}, u32[]{:S(2)}) collective-permute-start(bf16[2,1024,128]{2,1,0:T(8,128)(2,1)} %get-tuple-element.44), channel_id=1, source_target_pairs={{0,16},{16,0},{1,17},{17,1},{2,18},{18,2},{3,19},{19,3},{4,20},{20... | collective-permute-start | bytes 1572872 | tf_op jit(solution)/shard_map/ppermute | solution.py:291
  93.6 7.0 %copy-start.1 = (bf16[2,1024,128]{2,1,0:T(8,128)(2,1)S(1)}, bf16[2,1024,128]{2,1,0:T(8,128)(2,1)}, u32[]{:S(2)}) copy-start(bf16[2,1024,128]{2,1,0:T(8,128)(2,1)} %get-tuple-element.45) | copy-start | bytes 1572868
  93.6 22.3 %all-to-all-start.1 = ((bf16[16,128,128]{2,1,0:T(8,128)(2,1)}), bf16[16,128,128]{2,1,0:T(8,128)(2,1)S(1)}, u32[]{:S(2)}, u32[]{:S(2)}) async-start(bf16[16,128,128]{2,1,0:T(8,128)(2,1)} %get-tuple-element.25), calls=%async_computation.1 | async-start | bytes 1048576 | tf_op jit(solution)/shard_map/all_to_all | solution.py:298
  100.8 1.0 copy-start.2

commit v2 on v1

--- a/solution.py
+++ b/solution.py
@@ -36,7 +36,7 @@
     value_parts, refs = refs[:n_parts], refs[n_parts:]
     dq_ref, *refs = refs
     sums, refs = refs[:n_parts], refs[n_parts:]
-    held_ref, k_ref, v_ref, kt_ref, bias_ref, p_ref, gp_ref, dk_acc, dv_acc, sems = refs
+    held_ref, k_ref, v_ref, kt_ref, bias_ref, p_refs, gp_refs, dk_acc, dv_acc, sems = refs
 
     depth_id, seq_id = lax.axis_index("depth"), lax.axis_index("seq")
     shift = offsets_ref[depth_id]
@@ -76,7 +76,8 @@
     for copy in copies[n_parts:]:
         copy.wait()
 
-    def step(number, n_past):
+    def step(number, n_past, odd):
+        p_ref, gp_ref = p_refs[odd], gp_refs[odd]
         first_row = aligned(number * block, block)
         per_block = block // tok_rows
         held = pl.ds(number * per_block, per_block)
@@ -135,11 +136,15 @@
         )
 
     for number in range(past):
-        step(number, number)
-
-    @pl.loop(past, n_blocks)
-    def _(number):
-        step(number, past)
+        step(number, number, number % 2)
+
+    @pl.loop(0, (n_blocks - past) // 2)
+    def _(pair):
+        for n in range(2):
+            step(past + 2 * pair + n, past, n)
+
+    if (n_blocks - past) % 2:
+        step(n_blocks - 1, past, 0)
 
     for n in range(n_parts):
         sums[n][0] = (dk_acc[part_at(n), :] * SCALING).astype(jnp.bfloat16)
@@ -169,8 +174,8 @@
             pltpu.VMEM((seq_total, HEAD_DIM), bf16),
             pltpu.VMEM((HEAD_DIM, seq_total), bf16),
             pltpu.VMEM((past + 1, block, block), f32),
-            pltpu.VMEM((rows, block), f32),
-            pltpu.VMEM((rows, block), f32),
+            [pltpu.VMEM((rows, block), f32)] * 2,
+            [pltpu.VMEM((rows, block), f32)] * 2,
             pltpu.VMEM((seq_total, HEAD_DIM), f32),
             pltpu.VMEM((seq_total, HEAD_DIM), f32),
             pltpu.SemaphoreType.DMA((n_pieces + 2 * n_parts,)),

time: 118 us -> 118 us (level)
  no operation moved by 1% of the time
where the time goes in v2:
time: 118 us; the launch traced here: 117 us
  starting transfers between devices  55.6 us (47%)
  Pallas kernels  29.6 us (25%)
  waiting for transfers between devices  27.1 us (23%)
  local copies, waits for them, and re-layouts  2.42 us (2%)
  other arithmetic  1.36 us (1%)
    ppermute x15, starting transfers between devices, received(): lax.ppermute(sent[k], 'seq', [(i, i ^ k) for i in range(parts)])  34.2 us
    pallas_call x2, Pallas kernels, attention_backward(): pl.pallas_call(functools.partial(backward_kernel, block, past, n_blocks,...  23.6 us
    ppermute x15, waiting for transfers between devices, received(): lax.ppermute(sent[k], 'seq', [(i, i ^ k) for i in range(parts)])  14.3 us
    all_to_all x2, waiting for transfers between devices, on_device(): lax.all_to_all(dq, 'seq', split_axis=0, concat_axis=0, tiled=True)  12.8 us
    all_to_all x2, starting transfers between devices, on_device(): lax.all_to_all(dq, 'seq', split_axis=0, concat_axis=0, tiled=True)  11.7 us
    all_to_all x1, starting transfers between devices, received(): lax.all_to_all(sent, 'seq', split_axis=0, concat_axis=0, tiled=True)  8.48 us
    pallas_call x2, Pallas kernels, pack(): pl.pallas_call(kernel, in_specs=[pl.BlockSpec(memory_space=pl.ANY)] * 2,...  4.48 us
  transfers between devices with their start and end apart: 22, of which 8 were waited for; matrix products, arithmetic and copies ran while one was open for 1% of the time, Pallas kernels for 22%

profile of v2, /device:TPU:0, one launch (start us, length us, event | category | flops | bytes accessed | tf_op | source)
XLA Modules:
  0.0 117.3 jit_solution(18403936468275877862)
XLA Ops:
  0.6 2.2 %shard_map.85 = bf16[16,2,128,128]{3,2,1,0:T(8,128)(2,1)} custom-call(bf16[128,4096]{1,0:T(8,128)(2,1)} %bitcast.11, bf16[128,4096]{1,0:T(8,128)(2,1)} %bitcast.13), custom_call_target="tpu_custom_call" | custom-call | bytes 2097152 | tf_op jit(solution)/shard_map/pallas_call | solution.py:221
  2.9 0.0 copy-start.3
  2.9 0.0 copy-start.4
  2.9 8.5 %all-to-all-start = ((bf16[16,2,128,128]{3,2,1,0:T(8,128)(2,1)}), bf16[16,2,128,128]{3,2,1,0:T(8,128)(2,1)S(1)}, u32[]{:S(2)}, u32[]{:S(2)}) async-start(bf16[16,2,128,128]{3,2,1,0:T(8,128)(2,1)} %shard_map.85), calls=%async_computation | async-start | bytes 2097152 | tf_op jit(solution)/shard_map/all_to_all | solution.py:282
  11.4 0.1 collective-permute-start
  11.5 0.0 copy-done.4
  11.5 0.5 collective-permute-start.1
  12.0 2.2 %shard_map.87 = (bf16[2,128,128]{2,1,0:T(8,128)(2,1)}, bf16[2,128,128]{2,1,0:T(8,128)(2,1)}, bf16[2,128,128]{2,1,0:T(8,128)(2,1)}, bf16[2,128,128]{2,1,0:T(8,128...) custom-call(bf16[128,4096]{1,0:T(8,128)(2,1)} %bitcast.12, ...), custom_call_target="tpu_custom_call" | custom-call | bytes 2097152 | tf_op jit(solution)/shard_map/pallas_call | solution.py:221
  14.2 2.0 %collective-permute-start.2 = (bf16[2,128,128]{2,1,0:T(8,128)(2,1)}, bf16[2,128,128]{2,1,0:T(8,128)(2,1)S(1)}, u32[]{:S(2)}, u32[]{:S(2)}) collective-permute-start(bf16[2,128,128]{2,1,0:T(8,128)(2,1)} %get-tuple-element.27), channel_id=1, source_target_pairs={{0,1},{1,0},{2,3},{3,2},{4,5},{5,4},{6,7},{7,6},{8,9},{9,8},{10,11... | collective-permute-start | bytes 196616 | tf_op jit(solution)/shard_map/ppermute | solution.py:279
  16.2 1.5 %collective-permute-start.3 = (bf16[2,128,128]{2,1,0:T(8,128)(2,1)}, bf16[2,128,128]{2,1,0:T(8,128)(2,1)S(1)}, u32[]{:S(2)}, u32[]{:S(2)}) collective-permute-start(bf16[2,128,128]{2,1,0:T(8,128)(2,1)} %get-tuple-element.28), channel_id=1, source_target_pairs={{0,2},{1,3},{2,0},{3,1},{4,6},{5,7},{6,4},{7,5},{8,10},{9,11},{10,... | collective-permute-start | bytes 196616 | tf_op jit(solution)/shard_map/ppermute | solution.py:279
  17.7 0.1 collective-permute-start.4
  17.8 1.0 collective-permute-done.2.refs_3_
  18.8 1.9 %collective-permute-start.5 = (bf16[2,128,128]{2,1,0:T(8,128)(2,1)}, bf16[2,128,128]{2,1,0:T(8,128)(2,1)S(1)}, u32[]{:S(2)}, u32[]{:S(2)}) collective-permute-start(bf16[2,128,128]{2,1,0:T(8,128)(2,1)} %get-tuple-element.30), channel_id=1, source_target_pairs={{0,4},{1,5},{2,6},{3,7},{4,0},{5,1},{6,2},{7,3},{8,12},{9,13},{10,... | collective-permute-start | bytes 196616 | tf_op jit(solution)/shard_map/ppermute | solution.py:279
  20.7 2.4 %collective-permute-done.3.refs_4_ = bf16[2,128,128]{2,1,0:T(8,128)(2,1)S(1)} collective-permute-done((bf16[2,128,128]{2,1,0:T(8,128)(2,1)}, bf16[2,128,128]{2,1,0:T(8,128)(2,1)S(1)}, u32[]{:S(2)}, u32[]{:S(2)}) %collective-permute-start.3) | collective-permute-done | bytes 65568 | tf_op jit(solution)/shard_map/ppermute | solution.py:279
  23.1 1.0 collective-permute-start.6
  24.0 0.3 collective-permute-done.4.refs_5_
  24.3 3.0 %collective-permute-start.7 = (bf16[2,128,128]{2,1,0:T(8,128)(2,1)}, bf16[2,128,128]{2,1,0:T(8,128)(2,1)S(1)}, u32[]{:S(2)}, u32[]{:S(2)}) collective-permute-start(bf16[2,128,128]{2,1,0:T(8,128)(2,1)} %get-tuple-element.32), channel_id=1, source_target_pairs={{0,6},{1,7},{2,4},{3,5},{4,2},{5,3},{6,0},{7,1},{8,14},{9,15},{10,... | collective-permute-start | bytes 196616 | tf_op jit(solution)/shard_map/ppermute | solution.py:279
  27.4 3.7 %collective-permute-done.5.refs_6_ = bf16[2,128,128]{2,1,0:T(8,128)(2,1)S(1)} collective-permute-done((bf16[2,128,128]{2,1,0:T(8,128)(2,1)}, bf16[2,128,128]{2,1,0:T(8,128)(2,1)S(1)}, u32[]{:S(2)}, u32[]{:S(2)}) %collective-permute-start.5) | collective-permute-done | bytes 65568 | tf_op jit(solution)/shard_map/ppermute | solution.py:279
  31.0 4.6 %collective-permute-start.8 = (bf16[2,128,128]{2,1,0:T(8,128)(2,1)}, bf16[2,128,128]{2,1,0:T(8,128)(2,1)S(1)}, u32[]{:S(2)}, u32[]{:S(2)}) collective-permute-start(bf16[2,128,128]{2,1,0:T(8,128)(2,1)} %get-tuple-element.33), channel_id=1, source_target_pairs={{0,7},{1,6},{2,5},{3,4},{4,3},{5,2},{6,1},{7,0},{8,15},{9,14},{10,... | collective-permute-start | bytes 196616 | tf_op jit(solution)/shard_map/ppermute | solution.py:279
  35.7 0.0 collective-permute-done.6.refs_7_
  35.7 1.9 %collective-permute-start.9 = (bf16[2,128,128]{2,1,0:T(8,128)(2,1)}, bf16[2,128,128]{2,1,0:T(8,128)(2,1)S(1)}, u32[]{:S(2)}, u32[]{:S(2)}) collective-permute-start(bf16[2,128,128]{2,1,0:T(8,128)(2,1)} %get-tuple-element.34), channel_id=1, source_target_pairs={{0,8},{1,9},{2,10},{3,11},{4,12},{5,13},{6,14},{7,15},{8,0},{9,1},... | collective-permute-start | bytes 196616 | tf_op jit(solution)/shard_map/ppermute | solution.py:279
  37.6 0.0 collective-permute-done.7.refs_8_
  37.6 3.3 %collective-permute-start.10 = (bf16[2,128,128]{2,1,0:T(8,128)(2,1)}, bf16[2,128,128]{2,1,0:T(8,128)(2,1)S(1)}, u32[]{:S(2)}, u32[]{:S(2)}) collective-permute-start(bf16[2,128,128]{2,1,0:T(8,128)(2,1)} %get-tuple-element.35), channel_id=1, source_target_pairs={{0,9},{1,8},{2,11},{3,10},{4,13},{5,12},{6,15},{7,14},{8,1},{9,0},... | collective-permute-start | bytes 196616 | tf_op jit(solution)/shard_map/ppermute | solution.py:279
  40.8 0.0 collective-permute-done.8.refs_9_
  40.8 3.0 %collective-permute-start.11 = (bf16[2,128,128]{2,1,0:T(8,128)(2,1)}, bf16[2,128,128]{2,1,0:T(8,128)(2,1)S(1)}, u32[]{:S(2)}, u32[]{:S(2)}) collective-permute-start(bf16[2,128,128]{2,1,0:T(8,128)(2,1)} %get-tuple-element.36), channel_id=1, source_target_pairs={{0,10},{1,11},{2,8},{3,9},{4,14},{5,15},{6,12},{7,13},{8,2},{9,3},... | collective-permute-start | bytes 196616 | tf_op jit(solution)/shard_map/ppermute | solution.py:279
  43.8 0.0 collective-permute-done.9.refs_10_
  43.8 0.8 collective-permute-start.12
  44.6 0.0 collective-permute-done.10.refs_11_
  44.6 3.5 %collective-permute-start.13 = (bf16[2,128,128]{2,1,0:T(8,128)(2,1)}, bf16[2,128,128]{2,1,0:T(8,128)(2,1)S(1)}, u32[]{:S(2)}, u32[]{:S(2)}) collective-permute-start(bf16[2,128,128]{2,1,0:T(8,128)(2,1)} %get-tuple-element.38), channel_id=1, source_target_pairs={{0,12},{1,13},{2,14},{3,15},{4,8},{5,9},{6,10},{7,11},{8,4},{9,5},... | collective-permute-start | bytes 196616 | tf_op jit(solution)/shard_map/ppermute | solution.py:279
  48.1 2.0 %collective-permute-done.11.refs_12_ = bf16[2,128,128]{2,1,0:T(8,128)(2,1)S(1)} collective-permute-done((bf16[2,128,128]{2,1,0:T(8,128)(2,1)}, bf16[2,128,128]{2,1,0:T(8,128)(2,1)S(1)}, u32[]{:S(2)}, u32[]{:S(2)}) %collective-permute-start.11) | collective-permute-done | bytes 65568 | tf_op jit(solution)/shard_map/ppermute | solution.py:279
  50.1 2.6 %collective-permute-start.14 = (bf16[2,128,128]{2,1,0:T(8,128)(2,1)}, bf16[2,128,128]{2,1,0:T(8,128)(2,1)S(1)}, u32[]{:S(2)}, u32[]{:S(2)}) collective-permute-start(bf16[2,128,128]{2,1,0:T(8,128)(2,1)} %get-tuple-element.39), channel_id=1, source_target_pairs={{0,13},{1,12},{2,15},{3,14},{4,9},{5,8},{6,11},{7,10},{8,5},{9,4},... | collective-permute-start | bytes 196616 | tf_op jit(solution)/shard_map/ppermute | solution.py:279
  52.7 0.0 collective-permute-done.12.refs_13_
  52.7 2.0 %collective-permute-start.15 = (bf16[2,128,128]{2,1,0:T(8,128)(2,1)}, bf16[2,128,128]{2,1,0:T(8,128)(2,1)S(1)}, u32[]{:S(2)}, u32[]{:S(2)}) collective-permute-start(bf16[2,128,128]{2,1,0:T(8,128)(2,1)} %get-tuple-element.40), channel_id=1, source_target_pairs={{0,14},{1,15},{2,12},{3,13},{4,10},{5,11},{6,8},{7,9},{8,6},{9,7},... | collective-permute-start | bytes 196616 | tf_op jit(solution)/shard_map/ppermute | solution.py:279
  54.8 0.0 collective-permute-done.13.refs_14_
  54.8 3.1 %collective-permute-start.16 = (bf16[2,128,128]{2,1,0:T(8,128)(2,1)}, bf16[2,128,128]{2,1,0:T(8,128)(2,1)S(1)}, u32[]{:S(2)}, u32[]{:S(2)}) collective-permute-start(bf16[2,128,128]{2,1,0:T(8,128)(2,1)} %get-tuple-element.41), channel_id=1, source_target_pairs={{0,15},{1,14},{2,13},{3,12},{4,11},{5,10},{6,9},{7,8},{8,7},{9,6},... | collective-permute-start | bytes 196616 | tf_op jit(solution)/shard_map/ppermute | solution.py:279
  57.8 0.0 collective-permute-done.14.refs_15_
  57.8 2.0 %collective-permute-done.15.refs_16_ = bf16[2,128,128]{2,1,0:T(8,128)(2,1)S(1)} collective-permute-done((bf16[2,128,128]{2,1,0:T(8,128)(2,1)}, bf16[2,128,128]{2,1,0:T(8,128)(2,1)S(1)}, u32[]{:S(2)}, u32[]{:S(2)}) %collective-permute-start.15) | collective-permute-done | bytes 65568 | tf_op jit(solution)/shard_map/ppermute | solution.py:279
  59.9 2.9 %collective-permute-done.16.refs_17_ = bf16[2,128,128]{2,1,0:T(8,128)(2,1)S(1)} collective-permute-done((bf16[2,128,128]{2,1,0:T(8,128)(2,1)}, bf16[2,128,128]{2,1,0:T(8,128)(2,1)S(1)}, u32[]{:S(2)}, u32[]{:S(2)}) %collective-permute-start.16) | collective-permute-done | bytes 65568 | tf_op jit(solution)/shard_map/ppermute | solution.py:279
  62.8 0.0 collective-permute-done.refs_4_.refs_19_
  62.8 0.0 collective-permute-done.1.refs_6_.refs_21_
  62.9 0.5 copy-done.22
  63.5 0.0 copy-done.10
  63.5 0.0 copy-done.11
  63.5 0.0 copy-done.12
  63.5 0.0 copy-done.13
  63.5 0.1 copy-done.5
  63.7 0.6 copy-done.6
  64.3 11.8 %shard_map.88 = (bf16[16,128,128]{2,1,0:T(8,128)(2,1)}, bf16[2,1024,128]{2,1,0:T(8,128)(2,1)}, bf16[2,1024,128]{2,1,0:T(8,128)(2,1)}) custom-call(s32[2]{0:T(128)} %refs_0_.3, s32[2]{0:T(128)} %refs_1_.3, bf16[2,128,128]{2,1,0:T(8,128)(2,1)} %get-tuple-element.26.refs_2_, bf16[2,128,128]{2,1,0:T(8,128)(2,1)} %copy-done.8, bf16[2,128,128]{2,1,0:T(8,128)(2,1)} %copy-done.9, ...), custom_call_target="tpu_custom_call" | custom-call | flops 3397386240 | bytes 3670016 | tf_op jit(solution)/shard_map/pallas_call | solution.py:166
  76.0 0.0 all-to-all-done.refs_2_
  76.1 0.0 copy-start
  76.1 4.6 %all-to-all-start.2 = ((bf16[16,128,128]{2,1,0:T(8,128)(2,1)}), bf16[16,128,128]{2,1,0:T(8,128)(2,1)S(1)}, u32[]{:S(2)}, u32[]{:S(2)}) async-start(bf16[16,128,128]{2,1,0:T(8,128)(2,1)} %get-tuple-element.42), calls=%async_computation.2 | async-start | bytes 1048576 | tf_op jit(solution)/shard_map/all_to_all | solution.py:303
  80.7 0.1 collective-permute-start.18
  80.8 11.8 %shard_map.86 = (bf16[16,128,128]{2,1,0:T(8,128)(2,1)}, bf16[2,1024,128]{2,1,0:T(8,128)(2,1)}, bf16[2,1024,128]{2,1,0:T(8,128)(2,1)}) custom-call(s32[2]{0:T(128)} %refs_0_.3, s32[2]{0:T(128)} %refs_1_.3, bf16[16,2,128,128]{3,2,1,0:T(8,128)(2,1)} %copy-done, bf16[1024,256]{1,0:T(8,128)(2,1)} %refs_18_.1, bf16[1024,256]{1,0:T(8,128)(2,1)} %copy-done.5, ...), custom_call_target="tpu_custom_call" | custom-call | flops 3397386240 | bytes 3670016 | tf_op jit(solution)/shard_map/pallas_call | solution.py:166
  92.6 0.6 collective-permute-start.17
  93.2 0.0 all-to-all-done.2.refs_1_
  93.2 7.0 %all-to-all-start.1 = ((bf16[16,128,128]{2,1,0:T(8,128)(2,1)}), bf16[16,128,128]{2,1,0:T(8,128)(2,1)S(1)}, u32[]{:S(2)}, u32[]{:S(2)}) async-start(bf16[16,128,128]{2,1,0:T(8,128)(2,1)} %get-tuple-element.25), calls=%async_computation.1 | async-start | bytes 1048576 | tf_op jit(solution)/shard_map/all_to_all | solution.py:303
  100.2 0.0 collective-permute-done.18
  100.2 0.1 add_convert_fusion
  100.4 0.0 collective-permute-done.17
  100.4 1.0 copy-done.2
  101.4 0.1 add_convert_fusion.1
  101.6 1.1 pad_maximum_fusion
  102.7 12.8 %all-to-all-done.1.refs_0_ = bf16[16,128,128]{2,1,0:T(8,128)(2,1)S(1)} async-done(((bf16[16,128,128]{2,1,0:T(8,128)(2,1)}), bf16[16,128,128]{2,1,0:T(8,128)(2,1)S(1)}, u32[]{:S(2)}, u32[]{:S(2)}) %all-to-all-start.1) | async-done | bytes 524320 | tf_op jit(solution)/shard_map/all_to_all | solution.py:303
  115.5 1.6 %unpack.1 = bf16[128,4096]{1,0:T(8,128)(2,1)} custom-call(bf16[16,128,128]{2,1,0:T(8,128)(2,1)S(1)} %all-to-all-done.1.refs_0_, bf16[16,128,128]{2,1,0:T(8,128)(2,1)S(1)} %all-to-all-done.2.refs_1_), custom_call_target="tpu_custom_call" | custom-call | tf_op jit(solution)/shard_map/unpack/pallas_call | solution.py:255
  (36 shorter events, 0.1 us)
Async XLA Ops:
  2.9 8.5 %copy-start.3 = (bf16[1024,256]{1,0:T(8,128)(2,1)S(1)}, bf16[1024,256]{1,0:T(8,128)(2,1)}, u32[]{:S(2)}) copy-start(bf16[1024,256]{1,0:T(8,128)(2,1)} %refs_18_.1) | copy-start | bytes 1572868
  2.9 8.6 %copy-start.4 = (bf16[1024,256]{1,0:T(8,128)(2,1)S(1)}, bf16[1024,256]{1,0:T(8,128)(2,1)}, u32[]{:S(2)}) copy-start(bf16[1024,256]{1,0:T(8,128)(2,1)} %refs_20_.1) | copy-start | bytes 1572868
  2.9 73.1 %all-to-all-start = ((bf16[16,2,128,128]{3,2,1,0:T(8,128)(2,1)}), bf16[16,2,128,128]{3,2,1,0:T(8,128)(2,1)S(1)}, u32[]{:S(2)}, u32[]{:S(2)}) async-start(bf16[16,2,128,128]{3,2,1,0:T(8,128)(2,1)} %shard_map.85), calls=%async_computation | async-start | bytes 2097152 | tf_op jit(solution)/shard_map/all_to_all | solution.py:282
  11.4 51.4 %collective-permute-start = (bf16[1024,256]{1,0:T(8,128)(2,1)S(1)}, bf16[1024,256]{1,0:T(8,128)(2,1)S(1)}, u32[]{:S(2)}, u32[]{:S(2)}) collective-permute-start(bf16[1024,256]{1,0:T(8,128)(2,1)S(1)} %copy-done.3), channel_id=1, source_target_pairs={{0,16},{16,0},{1,17},{17,1},{2,18},{18,2},{3,19},{19,3},{4,20},{20... | collective-permute-start | bytes 1572872 | tf_op jit(solution)/shard_map/ppermute | solution.py:288
  11.5 51.3 %collective-permute-start.1 = (bf16[1024,256]{1,0:T(8,128)(2,1)S(1)}, bf16[1024,256]{1,0:T(8,128)(2,1)S(1)}, u32[]{:S(2)}, u32[]{:S(2)}) collective-permute-start(bf16[1024,256]{1,0:T(8,128)(2,1)S(1)} %copy-done.4), channel_id=1, source_target_pairs={{0,16},{16,0},{1,17},{17,1},{2,18},{18,2},{3,19},{19,3},{4,20},{20... | collective-permute-start | bytes 1572872 | tf_op jit(solution)/shard_map/ppermute | solution.py:289
  14.2 4.5 %collective-permute-start.2 = (bf16[2,128,128]{2,1,0:T(8,128)(2,1)}, bf16[2,128,128]{2,1,0:T(8,128)(2,1)S(1)}, u32[]{:S(2)}, u32[]{:S(2)}) collective-permute-start(bf16[2,128,128]{2,1,0:T(8,128)(2,1)} %get-tuple-element.27), channel_id=1, source_target_pairs={{0,1},{1,0},{2,3},{3,2},{4,5},{5,4},{6,7},{7,6},{8,9},{9,8},{10,11... | collective-permute-start | bytes 196616 | tf_op jit(solution)/shard_map/ppermute | solution.py:279
  16.2 6.8 %collective-permute-start.3 = (bf16[2,128,128]{2,1,0:T(8,128)(2,1)}, bf16[2,128,128]{2,1,0:T(8,128)(2,1)S(1)}, u32[]{:S(2)}, u32[]{:S(2)}) collective-permute-start(bf16[2,128,128]{2,1,0:T(8,128)(2,1)} %get-tuple-element.28), channel_id=1, source_target_pairs={{0,2},{1,3},{2,0},{3,1},{4,6},{5,7},{6,4},{7,5},{8,10},{9,11},{10,... | collective-permute-start | bytes 196616 | tf_op jit(solution)/shard_map/ppermute | solution.py:279
  17.7 6.7 %collective-permute-start.4 = (bf16[2,128,128]{2,1,0:T(8,128)(2,1)}, bf16[2,128,128]{2,1,0:T(8,128)(2,1)S(1)}, u32[]{:S(2)}, u32[]{:S(2)}) collective-permute-start(bf16[2,128,128]{2,1,0:T(8,128)(2,1)} %get-tuple-element.29), channel_id=1, source_target_pairs={{0,3},{1,2},{2,1},{3,0},{4,7},{5,6},{6,5},{7,4},{8,11},{9,10},{10,... | collective-permute-start | bytes 196616 | tf_op jit(solution)/shard_map/ppermute | solution.py:279
  18.8 44.7 %copy-start.8 = (bf16[2,128,128]{2,1,0:T(8,128)(2,1)}, bf16[2,128,128]{2,1,0:T(8,128)(2,1)S(1)}, u32[]{:S(2)}) copy-start(bf16[2,128,128]{2,1,0:T(8,128)(2,1)S(1)} %collective-permute-done.2.refs_3_) | copy-start | bytes 196612
  18.8 12.3 %collective-permute-start.5 = (bf16[2,128,128]{2,1,0:T(8,128)(2,1)}, bf16[2,128,128]{2,1,0:T(8,128)(2,1)S(1)}, u32[]{:S(2)}, u32[]{:S(2)}) collective-permute-start(bf16[2,128,128]{2,1,0:T(8,128)(2,1)} %get-tuple-element.30), channel_id=1, source_target_pairs={{0,4},{1,5},{2,6},{3,7},{4,0},{5,1},{6,2},{7,3},{8,12},{9,13},{10,... | collective-permute-start | bytes 196616 | tf_op jit(solution)/shard_map/ppermute | solution.py:279
  23.1 40.4 %copy-start.9 = (bf16[2,128,128]{2,1,0:T(8,128)(2,1)}, bf16[2,128,128]{2,1,0:T(8,128)(2,1)S(1)}, u32[]{:S(2)}) copy-start(bf16[2,128,128]{2,1,0:T(8,128)(2,1)S(1)} %collective-permute-done.3.refs_4_) | copy-start | bytes 196612
  23.1 12.6 %collective-permute-start.6 = (bf16[2,128,128]{2,1,0:T(8,128)(2,1)}, bf16[2,128,128]{2,1,0:T(8,128)(2,1)S(1)}, u32[]{:S(2)}, u32[]{:S(2)}) collective-permute-start(bf16[2,128,128]{2,1,0:T(8,128)(2,1)} %get-tuple-element.31), channel_id=1, source_target_pairs={{0,5},{1,4},{2,7},{3,6},{4,1},{5,0},{6,3},{7,2},{8,13},{9,12},{10,... | collective-permute-start | bytes 196616 | tf_op jit(solution)/shard_map/ppermute | solution.py:279
  24.3 39.1 %copy-start.10 = (bf16[2,128,128]{2,1,0:T(8,128)(2,1)}, bf16[2,128,128]{2,1,0:T(8,128)(2,1)S(1)}, u32[]{:S(2)}) copy-start(bf16[2,128,128]{2,1,0:T(8,128)(2,1)S(1)} %collective-permute-done.4.refs_5_) | copy-start | bytes 196612
  24.3 13.2 %collective-permute-start.7 = (bf16[2,128,128]{2,1,0:T(8,128)(2,1)}, bf16[2,128,128]{2,1,0:T(8,128)(2,1)S(1)}, u32[]{:S(2)}, u32[]{:S(2)}) collective-permute-start(bf16[2,128,128]{2,1,0:T(8,128)(2,1)} %get-tuple-element.32), channel_id=1, source_target_pairs={{0,6},{1,7},{2,4},{3,5},{4,2},{5,3},{6,0},{7,1},{8,14},{9,15},{10,... | collective-permute-start | bytes 196616 | tf_op jit(solution)/shard_map/ppermute | solution.py:279
  31.0 32.4 %copy-start.11 = (bf16[2,128,128]{2,1,0:T(8,128)(2,1)}, bf16[2,128,128]{2,1,0:T(8,128)(2,1)S(1)}, u32[]{:S(2)}) copy-start(bf16[2,128,128]{2,1,0:T(8,128)(2,1)S(1)} %collective-permute-done.5.refs_6_) | copy-start | bytes 196612
  31.0 9.8 %collective-permute-start.8 = (bf16[2,128,128]{2,1,0:T(8,128)(2,1)}, bf16[2,128,128]{2,1,0:T(8,128)(2,1)S(1)}, u32[]{:S(2)}, u32[]{:S(2)}) collective-permute-start(bf16[2,128,128]{2,1,0:T(8,128)(2,1)} %get-tuple-element.33), channel_id=1, source_target_pairs={{0,7},{1,6},{2,5},{3,4},{4,3},{5,2},{6,1},{7,0},{8,15},{9,14},{10,... | collective-permute-start | bytes 196616 | tf_op jit(solution)/shard_map/ppermute | solution.py:279
  35.7 27.8 %copy-start.12 = (bf16[2,128,128]{2,1,0:T(8,128)(2,1)}, bf16[2,128,128]{2,1,0:T(8,128)(2,1)S(1)}, u32[]{:S(2)}) copy-start(bf16[2,128,128]{2,1,0:T(8,128)(2,1)S(1)} %collective-permute-done.6.refs_7_) | copy-start | bytes 196612
  35.7 8.2 %collective-permute-start.9 = (bf16[2,128,128]{2,1,0:T(8,128)(2,1)}, bf16[2,128,128]{2,1,0:T(8,128)(2,1)S(1)}, u32[]{:S(2)}, u32[]{:S(2)}) collective-permute-start(bf16[2,128,128]{2,1,0:T(8,128)(2,1)} %get-tuple-element.34), channel_id=1, source_target_pairs={{0,8},{1,9},{2,10},{3,11},{4,12},{5,13},{6,14},{7,15},{8,0},{9,1},... | collective-permute-start | bytes 196616 | tf_op jit(solution)/shard_map/ppermute | solution.py:279
  37.6 25.9 %copy-start.13 = (bf16[2,128,128]{2,1,0:T(8,128)(2,1)}, bf16[2,128,128]{2,1,0:T(8,128)(2,1)S(1)}, u32[]{:S(2)}) copy-start(bf16[2,128,128]{2,1,0:T(8,128)(2,1)S(1)} %collective-permute-done.7.refs_8_) | copy-start | bytes 196612
  37.6 7.1 %collective-permute-start.10 = (bf16[2,128,128]{2,1,0:T(8,128)(2,1)}, bf16[2,128,128]{2,1,0:T(8,128)(2,1)S(1)}, u32[]{:S(2)}, u32[]{:S(2)}) collective-permute-start(bf16[2,128,128]{2,1,0:T(8,128)(2,1)} %get-tuple-element.35), channel_id=1, source_target_pairs={{0,9},{1,8},{2,11},{3,10},{4,13},{5,12},{6,15},{7,14},{8,1},{9,0},... | collective-permute-start | bytes 196616 | tf_op jit(solution)/shard_map/ppermute | solution.py:279
  40.8 22.0 %copy-start.14 = (bf16[2,128,128]{2,1,0:T(8,128)(2,1)}, bf16[2,128,128]{2,1,0:T(8,128)(2,1)S(1)}, u32[]{:S(2)}) copy-start(bf16[2,128,128]{2,1,0:T(8,128)(2,1)S(1)} %collective-permute-done.8.refs_9_) | copy-start | bytes 196612
  40.8 9.3 %collective-permute-start.11 = (bf16[2,128,128]{2,1,0:T(8,128)(2,1)}, bf16[2,128,128]{2,1,0:T(8,128)(2,1)S(1)}, u32[]{:S(2)}, u32[]{:S(2)}) collective-permute-start(bf16[2,128,128]{2,1,0:T(8,128)(2,1)} %get-tuple-element.36), channel_id=1, source_target_pairs={{0,10},{1,11},{2,8},{3,9},{4,14},{5,15},{6,12},{7,13},{8,2},{9,3},... | collective-permute-start | bytes 196616 | tf_op jit(solution)/shard_map/ppermute | solution.py:279
  43.8 19.0 %copy-start.15 = (bf16[2,128,128]{2,1,0:T(8,128)(2,1)}, bf16[2,128,128]{2,1,0:T(8,128)(2,1)S(1)}, u32[]{:S(2)}) copy-start(bf16[2,128,128]{2,1,0:T(8,128)(2,1)S(1)} %collective-permute-done.9.refs_10_) | copy-start | bytes 196612
  43.8 8.9 %collective-permute-start.12 = (bf16[2,128,128]{2,1,0:T(8,128)(2,1)}, bf16[2,128,128]{2,1,0:T(8,128)(2,1)S(1)}, u32[]{:S(2)}, u32[]{:S(2)}) collective-permute-start(bf16[2,128,128]{2,1,0:T(8,128)(2,1)} %get-tuple-element.37), channel_id=1, source_target_pairs={{0,11},{1,10},{2,9},{3,8},{4,15},{5,14},{6,13},{7,12},{8,3},{9,2},... | collective-permute-start | bytes 196616 | tf_op jit(solution)/shard_map/ppermute | solution.py:279
  44.6 18.3 %copy-start.16 = (bf16[2,128,128]{2,1,0:T(8,128)(2,1)}, bf16[2,128,128]{2,1,0:T(8,128)(2,1)S(1)}, u32[]{:S(2)}) copy-start(bf16[2,128,128]{2,1,0:T(8,128)(2,1)S(1)} %collective-permute-done.10.refs_11_) | copy-start | bytes 196612
  44.6 10.1 %collective-permute-start.13 = (bf16[2,128,128]{2,1,0:T(8,128)(2,1)}, bf16[2,128,128]{2,1,0:T(8,128)(2,1)S(1)}, u32[]{:S(2)}, u32[]{:S(2)}) collective-permute-start(bf16[2,128,128]{2,1,0:T(8,128)(2,1)} %get-tuple-element.38), channel_id=1, source_target_pairs={{0,12},{1,13},{2,14},{3,15},{4,8},{5,9},{6,10},{7,11},{8,4},{9,5},... | collective-permute-start | bytes 196616 | tf_op jit(solution)/shard_map/ppermute | solution.py:279
  50.1 12.8 %copy-start.17 = (bf16[2,128,128]{2,1,0:T(8,128)(2,1)}, bf16[2,128,128]{2,1,0:T(8,128)(2,1)S(1)}, u32[]{:S(2)}) copy-start(bf16[2,128,128]{2,1,0:T(8,128)(2,1)S(1)} %collective-permute-done.11.refs_12_) | copy-start | bytes 196612
  50.1 7.7 %collective-permute-start.14 = (bf16[2,128,128]{2,1,0:T(8,128)(2,1)}, bf16[2,128,128]{2,1,0:T(8,128)(2,1)S(1)}, u32[]{:S(2)}, u32[]{:S(2)}) collective-permute-start(bf16[2,128,128]{2,1,0:T(8,128)(2,1)} %get-tuple-element.39), channel_id=1, source_target_pairs={{0,13},{1,12},{2,15},{3,14},{4,9},{5,8},{6,11},{7,10},{8,5},{9,4},... | collective-permute-start | bytes 196616 | tf_op jit(solution)/shard_map/ppermute | solution.py:279
  52.7 10.2 %copy-start.18 = (bf16[2,128,128]{2,1,0:T(8,128)(2,1)}, bf16[2,128,128]{2,1,0:T(8,128)(2,1)S(1)}, u32[]{:S(2)}) copy-start(bf16[2,128,128]{2,1,0:T(8,128)(2,1)S(1)} %collective-permute-done.12.refs_13_) | copy-start | bytes 196612
  52.7 7.2 %collective-permute-start.15 = (bf16[2,128,128]{2,1,0:T(8,128)(2,1)}, bf16[2,128,128]{2,1,0:T(8,128)(2,1)S(1)}, u32[]{:S(2)}, u32[]{:S(2)}) collective-permute-start(bf16[2,128,128]{2,1,0:T(8,128)(2,1)} %get-tuple-element.40), channel_id=1, source_target_pairs={{0,14},{1,15},{2,12},{3,13},{4,10},{5,11},{6,8},{7,9},{8,6},{9,7},... | collective-permute-start | bytes 196616 | tf_op jit(solution)/shard_map/ppermute | solution.py:279
  54.8 8.1 %copy-start.19 = (bf16[2,128,128]{2,1,0:T(8,128)(2,1)}, bf16[2,128,128]{2,1,0:T(8,128)(2,1)S(1)}, u32[]{:S(2)}) copy-start(bf16[2,128,128]{2,1,0:T(8,128)(2,1)S(1)} %collective-permute-done.13.refs_14_) | copy-start | bytes 196612
  54.8 8.1 %collective-permute-start.16 = (bf16[2,128,128]{2,1,0:T(8,128)(2,1)}, bf16[2,128,128]{2,1,0:T(8,128)(2,1)S(1)}, u32[]{:S(2)}, u32[]{:S(2)}) collective-permute-start(bf16[2,128,128]{2,1,0:T(8,128)(2,1)} %get-tuple-element.41), channel_id=1, source_target_pairs={{0,15},{1,14},{2,13},{3,12},{4,11},{5,10},{6,9},{7,8},{8,7},{9,6},... | collective-permute-start | bytes 196616 | tf_op jit(solution)/shard_map/ppermute | solution.py:279
  57.8 5.1 %copy-start.20 = (bf16[2,128,128]{2,1,0:T(8,128)(2,1)}, bf16[2,128,128]{2,1,0:T(8,128)(2,1)S(1)}, u32[]{:S(2)}) copy-start(bf16[2,128,128]{2,1,0:T(8,128)(2,1)S(1)} %collective-permute-done.14.refs_15_) | copy-start | bytes 196612
  59.9 3.0 %copy-start.21 = (bf16[2,128,128]{2,1,0:T(8,128)(2,1)}, bf16[2,128,128]{2,1,0:T(8,128)(2,1)S(1)}, u32[]{:S(2)}) copy-start(bf16[2,128,128]{2,1,0:T(8,128)(2,1)S(1)} %collective-permute-done.15.refs_16_) | copy-start | bytes 196612
  62.8 0.6 copy-start.22
  62.8 0.8 copy-start.5
  63.5 0.8 copy-start.6
  76.1 4.8 %copy-start = (bf16[16,2,128,128]{3,2,1,0:T(8,128)(2,1)}, bf16[16,2,128,128]{3,2,1,0:T(8,128)(2,1)S(1)}, u32[]{:S(2)}) copy-start(bf16[16,2,128,128]{3,2,1,0:T(8,128)(2,1)S(1)} %all-to-all-done.refs_2_) | copy-start | bytes 3145732
  76.1 4.7 %copy-start.7 = (bf16[2,1024,128]{2,1,0:T(8,128)(2,1)S(1)}, bf16[2,1024,128]{2,1,0:T(8,128)(2,1)}, u32[]{:S(2)}) copy-start(bf16[2,1024,128]{2,1,0:T(8,128)(2,1)} %get-tuple-element.46) | copy-start | bytes 1572868
  76.1 17.1 %all-to-all-start.2 = ((bf16[16,128,128]{2,1,0:T(8,128)(2,1)}), bf16[16,128,128]{2,1,0:T(8,128)(2,1)S(1)}, u32[]{:S(2)}, u32[]{:S(2)}) async-start(bf16[16,128,128]{2,1,0:T(8,128)(2,1)} %get-tuple-element.42), calls=%async_computation.2 | async-start | bytes 1048576 | tf_op jit(solution)/shard_map/all_to_all | solution.py:303
  80.7 19.5 %collective-permute-start.18 = (bf16[2,1024,128]{2,1,0:T(8,128)(2,1)S(1)}, bf16[2,1024,128]{2,1,0:T(8,128)(2,1)S(1)}, u32[]{:S(2)}, u32[]{:S(2)}) collective-permute-start(bf16[2,1024,128]{2,1,0:T(8,128)(2,1)S(1)} %copy-done.7), channel_id=1, source_target_pairs={{0,16},{16,0},{1,17},{17,1},{2,18},{18,2},{3,19},{19,3},{4,20},{20... | collective-permute-start | bytes 1572872 | tf_op jit(solution)/shard_map/ppermute | solution.py:296
  92.6 7.8 %collective-permute-start.17 = (bf16[2,1024,128]{2,1,0:T(8,128)(2,1)}, bf16[2,1024,128]{2,1,0:T(8,128)(2,1)S(1)}, u32[]{:S(2)}, u32[]{:S(2)}) collective-permute-start(bf16[2,1024,128]{2,1,0:T(8,128)(2,1)} %get-tuple-element.44), channel_id=1, source_target_pairs={{0,16},{16,0},{1,17},{17,1},{2,18},{18,2},{3,19},{19,3},{4,20},{20... | collective-permute-start | bytes 1572872 | tf_op jit(solution)/shard_map/ppermute | solution.py:296
  93.2 7.1 %copy-start.1 = (bf16[2,1024,128]{2,1,0:T(8,128)(2,1)S(1)}, bf16[2,1024,128]{2,1,0:T(8,128)(2,1)}, u32[]{:S(2)}) copy-start(bf16[2,1024,128]{2,1,0:T(8,128)(2,1)} %get-tuple-element.45) | copy-start | bytes 1572868
  93.2 22.3 %all-to-all-start.1 = ((bf16[16,128,128]{2,1,0:T(8,128)(2,1)}), bf16[16,128,128]{2,1,0:T(8,128)(2,1)S(1)}, u32[]{:S(2)}, u32[]{:S(2)}) async-start(bf16[16,128,128]{2,1,0:T(8,128)(2,1)} %get-tuple-element.25), calls=%async_computation.1 | async-start | bytes 1048576 | tf_op jit(solution)/shard_map/all_to_all | solution.py:303
  100.4 1.0 copy-start.2

commit v3 on v2

--- a/solution.py
+++ b/solution.py
@@ -234,33 +234,32 @@
     )(queries, grad_out)
 
 
-def unpack(back, tok_rows, model_width):
-    heads = len(back)
-    parts = back[0].shape[0]
+def unpack(arrived, head, heads, tok_rows, so_far):
+    parts = arrived.shape[0]
 
     def kernel(*refs):
-        ins, out, sems = refs[:heads], refs[heads], refs[heads + 1]
-        copies = []
-        for head in range(heads):
-            for d in range(parts):
-                columns = pl.ds((d * heads + head) * HEAD_DIM, HEAD_DIM)
-                copies.append(
-                    pltpu.make_async_copy(ins[head].at[d], out.at[:, columns], sems.at[head, d])
-                )
+        source, out, sems = refs[0], refs[-2], refs[-1]
+        copies = [
+            pltpu.make_async_copy(
+                source.at[d], out.at[:, pl.ds((d * heads + head) * HEAD_DIM, HEAD_DIM)], sems.at[d]
+            )
+            for d in range(parts)
+        ]
         for copy in copies:
             copy.start()
         for copy in copies:
             copy.wait()
 
+    args = [arrived] if so_far is None else [arrived, so_far]
     return pl.pallas_call(
         kernel,
-        in_specs=[pl.BlockSpec(memory_space=pl.ANY)] * heads,
-        out_specs=pl.BlockSpec(memory_space=pltpu.VMEM),
-        out_shape=jax.ShapeDtypeStruct((tok_rows, model_width), jnp.bfloat16),
-        scratch_shapes=[pltpu.SemaphoreType.DMA((heads, parts))],
-        compiler_params=pltpu.CompilerParams(vmem_limit_bytes=8 * 2**20),
-        name="unpack",
-    )(*back)
+        in_specs=[pl.BlockSpec(memory_space=pl.ANY)] * len(args),
+        out_specs=pl.BlockSpec(memory_space=pl.ANY),
+        out_shape=jax.ShapeDtypeStruct((tok_rows, parts * heads * HEAD_DIM), jnp.bfloat16),
+        input_output_aliases={} if so_far is None else {1: 0},
+        scratch_shapes=[pltpu.SemaphoreType.DMA((parts,))],
+        compiler_params=pltpu.CompilerParams(vmem_limit_bytes=32 * 2**20),
+    )(*args)
 
 
 def on_device(queries, grad_out, key_states, value_states, offsets, windows):
@@ -303,8 +302,11 @@
         back.append(lax.all_to_all(dq, "seq", split_axis=0, concat_axis=0, tiled=True))
         totals.append(over_depths(sums))
 
+    whole = None
+    for head in range(heads):
+        whole = unpack(back[head], head, heads, tok_rows, whole)
     return (
-        unpack(back, tok_rows, model_width).reshape(1, tok_rows, model_width),
+        whole.reshape(1, tok_rows, model_width),
         jnp.concatenate([total[0] for total in totals], axis=1),
         jnp.concatenate([total[1] for total in totals], axis=1),
     )
@@ -320,6 +322,4 @@
         P(),
     )
     out_specs = (P("depth", "seq", None), P("depth", "seq"), P("depth", "seq"))
-    return jax.shard_map(
-        on_device, mesh=mesh, in_specs=in_specs, out_specs=out_specs, check_vma=False
-    )
+    return jax.shard_map(on_device, mesh=mesh, in_specs=in_specs, out_specs=out_specs, check_vma=False)

time: 118 us -> 126 us (1.068)
  waiting for transfers between devices: 27.1 us -> 36 us
  starting transfers between devices: 55.6 us -> 53.7 us
    all_to_all x1, waiting for transfers between devices: 0.01 us -> 15.2 us  [received(): lax.all_to_all(sent, 'seq', split_axis=0, concat_axis=0, tiled=True)]
    ppermute x15, waiting for transfers between devices: 14.3 us -> 8.85 us  [received(): lax.ppermute(sent[k], 'seq', [(i, i ^ k) for i in range(parts)])]
    ppermute x15, starting transfers between devices: 34.2 us -> 31.8 us  [received(): lax.ppermute(sent[k], 'seq', [(i, i ^ k) for i in range(parts)])]
    unnamed x46 -> x66, local copies, waits for them, and re-layouts: 2.35 us -> 2.57 us
  transfers between devices with their start and end apart: 22 -> 22, of which waited for: 8 -> 7; matrix products, arithmetic and copies ran while one was open for 1% -> 1% of each run, Pallas kernels for 22% -> 22%
where the time goes in v3:
time: 126 us; the launch traced here: 125 us
  starting transfers between devices  53.7 us (43%)
  waiting for transfers between devices  36 us (29%)
  Pallas kernels  30 us (24%)
  local copies, waits for them, and re-layouts  2.64 us (2%)
  other arithmetic  1.36 us (1%)
    ppermute x15, starting transfers between devices, received(): lax.ppermute(sent[k], 'seq', [(i, i ^ k) for i in range(parts)])  31.8 us
    pallas_call x2, Pallas kernels, attention_backward(): pl.pallas_call(functools.partial(backward_kernel, block, past, n_blocks,...  23.7 us
    all_to_all x1, waiting for transfers between devices, received(): lax.all_to_all(sent, 'seq', split_axis=0, concat_axis=0, tiled=True)  15.2 us
    all_to_all x2, starting transfers between devices, on_device(): lax.all_to_all(dq, 'seq', split_axis=0, concat_axis=0, tiled=True)  12.3 us
    all_to_all x2, waiting for transfers between devices, on_device(): lax.all_to_all(dq, 'seq', split_axis=0, concat_axis=0, tiled=True)  11.9 us
    ppermute x15, waiting for transfers between devices, received(): lax.ppermute(sent[k], 'seq', [(i, i ^ k) for i in range(parts)])  8.85 us
    all_to_all x1, starting transfers between devices, received(): lax.all_to_all(sent, 'seq', split_axis=0, concat_axis=0, tiled=True)  8.48 us
    pallas_call x2, Pallas kernels, pack(): pl.pallas_call(kernel, in_specs=[pl.BlockSpec(memory_space=pl.ANY)] * 2,...  4.51 us
  transfers between devices with their start and end apart: 22, of which 7 were waited for; matrix products, arithmetic and copies ran while one was open for 1% of the time, Pallas kernels for 22%

profile of v3, /device:TPU:0, one launch (start us, length us, event | category | flops | bytes accessed | tf_op | source)
XLA Modules:
  0.0 124.9 jit_solution(12643775692580054354)
XLA Ops:
  0.6 2.2 %shard_map.87 = bf16[16,2,128,128]{3,2,1,0:T(8,128)(2,1)} custom-call(bf16[128,4096]{1,0:T(8,128)(2,1)} %bitcast.11, bf16[128,4096]{1,0:T(8,128)(2,1)} %bitcast.13), custom_call_target="tpu_custom_call" | custom-call | bytes 2097152 | tf_op jit(solution)/shard_map/pallas_call | solution.py:221
  2.9 0.0 copy-start.3
  2.9 0.0 copy-start.4
  2.9 8.5 %all-to-all-start.1 = ((bf16[16,2,128,128]{3,2,1,0:T(8,128)(2,1)}), bf16[16,2,128,128]{3,2,1,0:T(8,128)(2,1)S(1)}, u32[]{:S(2)}, u32[]{:S(2)}) async-start(bf16[16,2,128,128]{3,2,1,0:T(8,128)(2,1)} %shard_map.87), calls=%async_computation.1 | async-start | bytes 2097152 | tf_op jit(solution)/shard_map/all_to_all | solution.py:281
  11.4 0.1 collective-permute-start.15
  11.5 0.0 copy-done.4
  11.5 0.5 collective-permute-start.16
  12.0 2.3 %shard_map.85 = (bf16[2,128,128]{2,1,0:T(8,128)(2,1)}, bf16[2,128,128]{2,1,0:T(8,128)(2,1)}, bf16[2,128,128]{2,1,0:T(8,128)(2,1)}, bf16[2,128,128]{2,1,0:T(8,128...) custom-call(bf16[128,4096]{1,0:T(8,128)(2,1)} %bitcast.12, ...), custom_call_target="tpu_custom_call" | custom-call | bytes 2097152 | tf_op jit(solution)/shard_map/pallas_call | solution.py:221
  14.3 2.0 %collective-permute-start = (bf16[2,128,128]{2,1,0:T(8,128)(2,1)}, bf16[2,128,128]{2,1,0:T(8,128)(2,1)S(1)}, u32[]{:S(2)}, u32[]{:S(2)}) collective-permute-start(bf16[2,128,128]{2,1,0:T(8,128)(2,1)} %get-tuple-element.26), channel_id=1, source_target_pairs={{0,1},{1,0},{2,3},{3,2},{4,5},{5,4},{6,7},{7,6},{8,9},{9,8},{10,11... | collective-permute-start | bytes 196616 | tf_op jit(solution)/shard_map/ppermute | solution.py:278
  16.2 1.5 %collective-permute-start.1 = (bf16[2,128,128]{2,1,0:T(8,128)(2,1)}, bf16[2,128,128]{2,1,0:T(8,128)(2,1)S(1)}, u32[]{:S(2)}, u32[]{:S(2)}) collective-permute-start(bf16[2,128,128]{2,1,0:T(8,128)(2,1)} %get-tuple-element.27), channel_id=1, source_target_pairs={{0,2},{1,3},{2,0},{3,1},{4,6},{5,7},{6,4},{7,5},{8,10},{9,11},{10,... | collective-permute-start | bytes 196616 | tf_op jit(solution)/shard_map/ppermute | solution.py:278
  17.7 2.4 %collective-permute-start.10 = (bf16[2,128,128]{2,1,0:T(8,128)(2,1)}, bf16[2,128,128]{2,1,0:T(8,128)(2,1)S(1)}, u32[]{:S(2)}, u32[]{:S(2)}) collective-permute-start(bf16[2,128,128]{2,1,0:T(8,128)(2,1)} %get-tuple-element.36), channel_id=1, source_target_pairs={{0,11},{1,10},{2,9},{3,8},{4,15},{5,14},{6,13},{7,12},{8,3},{9,2},... | collective-permute-start | bytes 196616 | tf_op jit(solution)/shard_map/ppermute | solution.py:278
  20.1 0.0 collective-permute-done.15.refs_19_.refs_4_
  20.1 1.5 %collective-permute-start.11 = (bf16[2,128,128]{2,1,0:T(8,128)(2,1)}, bf16[2,128,128]{2,1,0:T(8,128)(2,1)S(1)}, u32[]{:S(2)}, u32[]{:S(2)}) collective-permute-start(bf16[2,128,128]{2,1,0:T(8,128)(2,1)} %get-tuple-element.37), channel_id=1, source_target_pairs={{0,12},{1,13},{2,14},{3,15},{4,8},{5,9},{6,10},{7,11},{8,4},{9,5},... | collective-permute-start | bytes 196616 | tf_op jit(solution)/shard_map/ppermute | solution.py:278
  21.5 0.0 collective-permute-done.16.refs_21_.refs_6_
  21.5 3.3 %collective-permute-start.12 = (bf16[2,128,128]{2,1,0:T(8,128)(2,1)}, bf16[2,128,128]{2,1,0:T(8,128)(2,1)S(1)}, u32[]{:S(2)}, u32[]{:S(2)}) collective-permute-start(bf16[2,128,128]{2,1,0:T(8,128)(2,1)} %get-tuple-element.38), channel_id=1, source_target_pairs={{0,13},{1,12},{2,15},{3,14},{4,9},{5,8},{6,11},{7,10},{8,5},{9,4},... | collective-permute-start | bytes 196616 | tf_op jit(solution)/shard_map/ppermute | solution.py:278
  24.8 15.2 %all-to-all-done.1.refs_2_ = bf16[16,2,128,128]{3,2,1,0:T(8,128)(2,1)S(1)} async-done(((bf16[16,2,128,128]{3,2,1,0:T(8,128)(2,1)}), bf16[16,2,128,128]{3,2,1,0:T(8,128)(2,1)S(1)}, u32[]{:S(2)}, u32[]{:S(2)}) %all-to-all-start.1) | async-done | bytes 1048608 | tf_op jit(solution)/shard_map/all_to_all | solution.py:281
  40.0 0.0 copy-done.5
  40.0 1.0 copy-done
  41.0 11.8 %shard_map.88 = (bf16[16,128,128]{2,1,0:T(8,128)(2,1)}, bf16[2,1024,128]{2,1,0:T(8,128)(2,1)}, bf16[2,1024,128]{2,1,0:T(8,128)(2,1)}) custom-call(s32[2]{0:T(128)} %refs_0_.3, s32[2]{0:T(128)} %refs_1_.3, bf16[16,2,128,128]{3,2,1,0:T(8,128)(2,1)} %copy-done, bf16[1024,256]{1,0:T(8,128)(2,1)} %refs_3_.1, bf16[1024,256]{1,0:T(8,128)(2,1)} %copy-done.5, ...), custom_call_target="tpu_custom_call" | custom-call | flops 3397386240 | bytes 3670016 | tf_op jit(solution)/shard_map/pallas_call | solution.py:166
  52.9 7.4 %all-to-all-start.2 = ((bf16[16,128,128]{2,1,0:T(8,128)(2,1)}), bf16[16,128,128]{2,1,0:T(8,128)(2,1)S(1)}, u32[]{:S(2)}, u32[]{:S(2)}) async-start(bf16[16,128,128]{2,1,0:T(8,128)(2,1)} %get-tuple-element.42), calls=%async_computation.2 | async-start | bytes 1048576 | tf_op jit(solution)/shard_map/all_to_all | solution.py:302
  60.3 0.0 collective-permute-done.refs_3_
  60.4 4.7 %collective-permute-start.13 = (bf16[2,128,128]{2,1,0:T(8,128)(2,1)S(1)}, bf16[2,128,128]{2,1,0:T(8,128)(2,1)S(1)}, u32[]{:S(2)}, u32[]{:S(2)}) collective-permute-start(bf16[2,128,128]{2,1,0:T(8,128)(2,1)S(1)} %copy-done.24), channel_id=1, source_target_pairs={{0,14},{1,15},{2,12},{3,13},{4,10},{5,11},{6,8},{7,9},{8,6},{9,7},... | collective-permute-start | bytes 196616 | tf_op jit(solution)/shard_map/ppermute | solution.py:278
  65.0 0.0 collective-permute-done.1.refs_4_
  65.0 1.5 %collective-permute-start.14 = (bf16[2,128,128]{2,1,0:T(8,128)(2,1)S(1)}, bf16[2,128,128]{2,1,0:T(8,128)(2,1)S(1)}, u32[]{:S(2)}, u32[]{:S(2)}) collective-permute-start(bf16[2,128,128]{2,1,0:T(8,128)(2,1)S(1)} %copy-done.22), channel_id=1, source_target_pairs={{0,15},{1,14},{2,13},{3,12},{4,11},{5,10},{6,9},{7,8},{8,7},{9,6},... | collective-permute-start | bytes 196616 | tf_op jit(solution)/shard_map/ppermute | solution.py:278
  66.6 0.0 collective-permute-done.10.refs_13_
  66.6 1.5 %collective-permute-start.2 = (bf16[2,128,128]{2,1,0:T(8,128)(2,1)S(1)}, bf16[2,128,128]{2,1,0:T(8,128)(2,1)S(1)}, u32[]{:S(2)}, u32[]{:S(2)}) collective-permute-start(bf16[2,128,128]{2,1,0:T(8,128)(2,1)S(1)} %copy-done.20), channel_id=1, source_target_pairs={{0,3},{1,2},{2,1},{3,0},{4,7},{5,6},{6,5},{7,4},{8,11},{9,10},{10,... | collective-permute-start | bytes 196616 | tf_op jit(solution)/shard_map/ppermute | solution.py:278
  68.1 0.0 collective-permute-done.11.refs_14_
  68.1 0.1 collective-permute-start.3
  68.2 0.0 collective-permute-done.12.refs_15_
  68.2 0.0 copy-start.17
  68.2 0.0 copy-done.18
  68.2 3.0 %collective-permute-start.4 = (bf16[2,128,128]{2,1,0:T(8,128)(2,1)S(1)}, bf16[2,128,128]{2,1,0:T(8,128)(2,1)S(1)}, u32[]{:S(2)}, u32[]{:S(2)}) collective-permute-start(bf16[2,128,128]{2,1,0:T(8,128)(2,1)S(1)} %copy-done.18), channel_id=1, source_target_pairs={{0,5},{1,4},{2,7},{3,6},{4,1},{5,0},{6,3},{7,2},{8,13},{9,12},{10,... | collective-permute-start | bytes 196616 | tf_op jit(solution)/shard_map/ppermute | solution.py:278
  71.2 3.8 %collective-permute-done.13.refs_16_ = bf16[2,128,128]{2,1,0:T(8,128)(2,1)S(1)} collective-permute-done((bf16[2,128,128]{2,1,0:T(8,128)(2,1)S(1)}, bf16[2,128,128]{2,1,0:T(8,128)(2,1)S(1)}, u32[]{:S(2)}, u32[]{:S(2)}) %collective-permute-start.13) | collective-permute-done | bytes 65568 | tf_op jit(solution)/shard_map/ppermute | solution.py:278
  75.0 4.1 %collective-permute-start.5 = (bf16[2,128,128]{2,1,0:T(8,128)(2,1)S(1)}, bf16[2,128,128]{2,1,0:T(8,128)(2,1)S(1)}, u32[]{:S(2)}, u32[]{:S(2)}) collective-permute-start(bf16[2,128,128]{2,1,0:T(8,128)(2,1)S(1)} %copy-done.16), channel_id=1, source_target_pairs={{0,6},{1,7},{2,4},{3,5},{4,2},{5,3},{6,0},{7,1},{8,14},{9,15},{10,... | collective-permute-start | bytes 196616 | tf_op jit(solution)/shard_map/ppermute | solution.py:278
  79.1 0.0 collective-permute-done.14.refs_17_
  79.1 1.6 %collective-permute-start.6 = (bf16[2,128,128]{2,1,0:T(8,128)(2,1)S(1)}, bf16[2,128,128]{2,1,0:T(8,128)(2,1)S(1)}, u32[]{:S(2)}, u32[]{:S(2)}) collective-permute-start(bf16[2,128,128]{2,1,0:T(8,128)(2,1)S(1)} %copy-done.15), channel_id=1, source_target_pairs={{0,7},{1,6},{2,5},{3,4},{4,3},{5,2},{6,1},{7,0},{8,15},{9,14},{10,... | collective-permute-start | bytes 196616 | tf_op jit(solution)/shard_map/ppermute | solution.py:278
  80.7 0.0 collective-permute-done.2.refs_5_
  80.7 0.0 copy-done.13
  80.7 1.7 %collective-permute-start.7 = (bf16[2,128,128]{2,1,0:T(8,128)(2,1)S(1)}, bf16[2,128,128]{2,1,0:T(8,128)(2,1)S(1)}, u32[]{:S(2)}, u32[]{:S(2)}) collective-permute-start(bf16[2,128,128]{2,1,0:T(8,128)(2,1)S(1)} %copy-done.13), channel_id=1, source_target_pairs={{0,8},{1,9},{2,10},{3,11},{4,12},{5,13},{6,14},{7,15},{8,0},{9,1},... | collective-permute-start | bytes 196616 | tf_op jit(solution)/shard_map/ppermute | solution.py:278
  82.4 0.0 collective-permute-done.3.refs_6_
  82.4 1.9 %collective-permute-start.8 = (bf16[2,128,128]{2,1,0:T(8,128)(2,1)S(1)}, bf16[2,128,128]{2,1,0:T(8,128)(2,1)S(1)}, u32[]{:S(2)}, u32[]{:S(2)}) collective-permute-start(bf16[2,128,128]{2,1,0:T(8,128)(2,1)S(1)} %copy-done.12), channel_id=1, source_target_pairs={{0,9},{1,8},{2,11},{3,10},{4,13},{5,12},{6,15},{7,14},{8,1},{9,0},... | collective-permute-start | bytes 196616 | tf_op jit(solution)/shard_map/ppermute | solution.py:278
  84.3 0.0 collective-permute-done.4.refs_7_
  84.3 1.3 %collective-permute-start.9 = (bf16[2,128,128]{2,1,0:T(8,128)(2,1)S(1)}, bf16[2,128,128]{2,1,0:T(8,128)(2,1)S(1)}, u32[]{:S(2)}, u32[]{:S(2)}) collective-permute-start(bf16[2,128,128]{2,1,0:T(8,128)(2,1)S(1)} %copy-done.10), channel_id=1, source_target_pairs={{0,10},{1,11},{2,8},{3,9},{4,14},{5,15},{6,12},{7,13},{8,2},{9,3},... | collective-permute-start | bytes 196616 | tf_op jit(solution)/shard_map/ppermute | solution.py:278
  85.6 0.0 collective-permute-done.5.refs_8_
  85.6 0.6 collective-permute-done.6.refs_9_
  86.2 0.3 collective-permute-done.7.refs_10_
  86.5 3.0 %collective-permute-done.8.refs_11_ = bf16[2,128,128]{2,1,0:T(8,128)(2,1)S(1)} collective-permute-done((bf16[2,128,128]{2,1,0:T(8,128)(2,1)S(1)}, bf16[2,128,128]{2,1,0:T(8,128)(2,1)S(1)}, u32[]{:S(2)}, u32[]{:S(2)}) %collective-permute-start.8) | collective-permute-done | bytes 65568 | tf_op jit(solution)/shard_map/ppermute | solution.py:278
  89.5 1.1 collective-permute-done.9.refs_12_
  90.6 0.0 copy-done.9
  90.7 0.5 copy-done.32
  91.2 11.9 %shard_map.86 = (bf16[16,128,128]{2,1,0:T(8,128)(2,1)}, bf16[2,1024,128]{2,1,0:T(8,128)(2,1)}, bf16[2,1024,128]{2,1,0:T(8,128)(2,1)}) custom-call(s32[2]{0:T(128)} %refs_0_.3, s32[2]{0:T(128)} %refs_1_.3, bf16[2,128,128]{2,1,0:T(8,128)(2,1)} %get-tuple-element.25.refs_2_, bf16[2,128,128]{2,1,0:T(8,128)(2,1)} %copy-done.8, bf16[2,128,128]{2,1,0:T(8,128)(2,1)} %copy-done.9, ...), custom_call_target="tpu_custom_call" | custom-call | flops 3397386240 | bytes 3670016 | tf_op jit(solution)/shard_map/pallas_call | solution.py:166
  103.1 0.1 collective-permute-start.18
  103.2 0.5 collective-permute-start.17
  103.7 0.0 all-to-all-done.2.refs_0_
  103.7 4.9 %all-to-all-start = ((bf16[16,128,128]{2,1,0:T(8,128)(2,1)}), bf16[16,128,128]{2,1,0:T(8,128)(2,1)S(1)}, u32[]{:S(2)}, u32[]{:S(2)}) async-start(bf16[16,128,128]{2,1,0:T(8,128)(2,1)} %get-tuple-element.41), calls=%async_computation | async-start | bytes 1048576 | tf_op jit(solution)/shard_map/all_to_all | solution.py:302
  108.5 0.0 collective-permute-done.18
  108.6 0.1 add_convert_fusion
  108.8 0.0 collective-permute-done.17
  108.8 1.0 copy-done.1
  109.8 0.1 add_convert_fusion.1
  109.9 1.1 pad_maximum_fusion
  111.0 0.9 shard_map.89.refs_1_
  111.9 11.9 %all-to-all-done.refs_0_ = bf16[16,128,128]{2,1,0:T(8,128)(2,1)S(1)} async-done(((bf16[16,128,128]{2,1,0:T(8,128)(2,1)}), bf16[16,128,128]{2,1,0:T(8,128)(2,1)S(1)}, u32[]{:S(2)}, u32[]{:S(2)}) %all-to-all-start) | async-done | bytes 524320 | tf_op jit(solution)/shard_map/all_to_all | solution.py:302
  123.9 0.9 shard_map.90
  (57 shorter events, 0.2 us)
Async XLA Ops:
  2.9 8.5 %copy-start.3 = (bf16[1024,256]{1,0:T(8,128)(2,1)S(1)}, bf16[1024,256]{1,0:T(8,128)(2,1)}, u32[]{:S(2)}) copy-start(bf16[1024,256]{1,0:T(8,128)(2,1)} %refs_3_.1) | copy-start | bytes 1572868
  2.9 8.6 %copy-start.4 = (bf16[1024,256]{1,0:T(8,128)(2,1)S(1)}, bf16[1024,256]{1,0:T(8,128)(2,1)}, u32[]{:S(2)}) copy-start(bf16[1024,256]{1,0:T(8,128)(2,1)} %refs_5_.1) | copy-start | bytes 1572868
  2.9 37.1 %all-to-all-start.1 = ((bf16[16,2,128,128]{3,2,1,0:T(8,128)(2,1)}), bf16[16,2,128,128]{3,2,1,0:T(8,128)(2,1)S(1)}, u32[]{:S(2)}, u32[]{:S(2)}) async-start(bf16[16,2,128,128]{3,2,1,0:T(8,128)(2,1)} %shard_map.87), calls=%async_computation.1 | async-start | bytes 2097152 | tf_op jit(solution)/shard_map/all_to_all | solution.py:281
  11.4 8.7 %collective-permute-start.15 = (bf16[1024,256]{1,0:T(8,128)(2,1)S(1)}, bf16[1024,256]{1,0:T(8,128)(2,1)S(1)}, u32[]{:S(2)}, u32[]{:S(2)}) collective-permute-start(bf16[1024,256]{1,0:T(8,128)(2,1)S(1)} %copy-done.3), channel_id=1, source_target_pairs={{0,16},{16,0},{1,17},{17,1},{2,18},{18,2},{3,19},{19,3},{4,20},{20... | collective-permute-start | bytes 1572872 | tf_op jit(solution)/shard_map/ppermute | solution.py:287
  11.5 10.0 %collective-permute-start.16 = (bf16[1024,256]{1,0:T(8,128)(2,1)S(1)}, bf16[1024,256]{1,0:T(8,128)(2,1)S(1)}, u32[]{:S(2)}, u32[]{:S(2)}) collective-permute-start(bf16[1024,256]{1,0:T(8,128)(2,1)S(1)} %copy-done.4), channel_id=1, source_target_pairs={{0,16},{16,0},{1,17},{17,1},{2,18},{18,2},{3,19},{19,3},{4,20},{20... | collective-permute-start | bytes 1572872 | tf_op jit(solution)/shard_map/ppermute | solution.py:288
  14.3 46.1 %collective-permute-start = (bf16[2,128,128]{2,1,0:T(8,128)(2,1)}, bf16[2,128,128]{2,1,0:T(8,128)(2,1)S(1)}, u32[]{:S(2)}, u32[]{:S(2)}) collective-permute-start(bf16[2,128,128]{2,1,0:T(8,128)(2,1)} %get-tuple-element.26), channel_id=1, source_target_pairs={{0,1},{1,0},{2,3},{3,2},{4,5},{5,4},{6,7},{7,6},{8,9},{9,8},{10,11... | collective-permute-start | bytes 196616 | tf_op jit(solution)/shard_map/ppermute | solution.py:278
  16.2 48.8 %collective-permute-start.1 = (bf16[2,128,128]{2,1,0:T(8,128)(2,1)}, bf16[2,128,128]{2,1,0:T(8,128)(2,1)S(1)}, u32[]{:S(2)}, u32[]{:S(2)}) collective-permute-start(bf16[2,128,128]{2,1,0:T(8,128)(2,1)} %get-tuple-element.27), channel_id=1, source_target_pairs={{0,2},{1,3},{2,0},{3,1},{4,6},{5,7},{6,4},{7,5},{8,10},{9,11},{10,... | collective-permute-start | bytes 196616 | tf_op jit(solution)/shard_map/ppermute | solution.py:278
  17.7 48.9 %collective-permute-start.10 = (bf16[2,128,128]{2,1,0:T(8,128)(2,1)}, bf16[2,128,128]{2,1,0:T(8,128)(2,1)S(1)}, u32[]{:S(2)}, u32[]{:S(2)}) collective-permute-start(bf16[2,128,128]{2,1,0:T(8,128)(2,1)} %get-tuple-element.36), channel_id=1, source_target_pairs={{0,11},{1,10},{2,9},{3,8},{4,15},{5,14},{6,13},{7,12},{8,3},{9,2},... | collective-permute-start | bytes 196616 | tf_op jit(solution)/shard_map/ppermute | solution.py:278
  20.1 19.9 %copy-start.5 = (bf16[1024,256]{1,0:T(8,128)(2,1)}, bf16[1024,256]{1,0:T(8,128)(2,1)S(1)}, u32[]{:S(2)}) copy-start(bf16[1024,256]{1,0:T(8,128)(2,1)S(1)} %collective-permute-done.15.refs_19_.refs_4_) | copy-start | bytes 1572868
  20.1 48.0 %collective-permute-start.11 = (bf16[2,128,128]{2,1,0:T(8,128)(2,1)}, bf16[2,128,128]{2,1,0:T(8,128)(2,1)S(1)}, u32[]{:S(2)}, u32[]{:S(2)}) collective-permute-start(bf16[2,128,128]{2,1,0:T(8,128)(2,1)} %get-tuple-element.37), channel_id=1, source_target_pairs={{0,12},{1,13},{2,14},{3,15},{4,8},{5,9},{6,10},{7,11},{8,4},{9,5},... | collective-permute-start | bytes 196616 | tf_op jit(solution)/shard_map/ppermute | solution.py:278
  21.5 18.5 %copy-start.6 = (bf16[1024,256]{1,0:T(8,128)(2,1)}, bf16[1024,256]{1,0:T(8,128)(2,1)S(1)}, u32[]{:S(2)}) copy-start(bf16[1024,256]{1,0:T(8,128)(2,1)S(1)} %collective-permute-done.16.refs_21_.refs_6_) | copy-start | bytes 1572868
  21.5 46.6 %collective-permute-start.12 = (bf16[2,128,128]{2,1,0:T(8,128)(2,1)}, bf16[2,128,128]{2,1,0:T(8,128)(2,1)S(1)}, u32[]{:S(2)}, u32[]{:S(2)}) collective-permute-start(bf16[2,128,128]{2,1,0:T(8,128)(2,1)} %get-tuple-element.38), channel_id=1, source_target_pairs={{0,13},{1,12},{2,15},{3,14},{4,9},{5,8},{6,11},{7,10},{8,5},{9,4},... | collective-permute-start | bytes 196616 | tf_op jit(solution)/shard_map/ppermute | solution.py:278
  40.0 1.0 copy-start
  52.8 7.6 %copy-start.24 = (bf16[2,128,128]{2,1,0:T(8,128)(2,1)S(1)}, bf16[2,128,128]{2,1,0:T(8,128)(2,1)}, u32[]{:S(2)}) copy-start(bf16[2,128,128]{2,1,0:T(8,128)(2,1)} %get-tuple-element.39) | copy-start | bytes 196612
  52.8 12.3 %copy-start.22 = (bf16[2,128,128]{2,1,0:T(8,128)(2,1)S(1)}, bf16[2,128,128]{2,1,0:T(8,128)(2,1)}, u32[]{:S(2)}) copy-start(bf16[2,128,128]{2,1,0:T(8,128)(2,1)} %get-tuple-element.40) | copy-start | bytes 196612
  52.8 13.8 %copy-start.20 = (bf16[2,128,128]{2,1,0:T(8,128)(2,1)S(1)}, bf16[2,128,128]{2,1,0:T(8,128)(2,1)}, u32[]{:S(2)}) copy-start(bf16[2,128,128]{2,1,0:T(8,128)(2,1)} %get-tuple-element.28) | copy-start | bytes 196612
  52.8 15.3 %copy-start.19 = (bf16[2,128,128]{2,1,0:T(8,128)(2,1)S(1)}, bf16[2,128,128]{2,1,0:T(8,128)(2,1)}, u32[]{:S(2)}) copy-start(bf16[2,128,128]{2,1,0:T(8,128)(2,1)} %get-tuple-element.29) | copy-start | bytes 196612
  52.8 15.4 %copy-start.18 = (bf16[2,128,128]{2,1,0:T(8,128)(2,1)S(1)}, bf16[2,128,128]{2,1,0:T(8,128)(2,1)}, u32[]{:S(2)}) copy-start(bf16[2,128,128]{2,1,0:T(8,128)(2,1)} %get-tuple-element.30) | copy-start | bytes 196612
  52.8 22.2 %copy-start.16 = (bf16[2,128,128]{2,1,0:T(8,128)(2,1)S(1)}, bf16[2,128,128]{2,1,0:T(8,128)(2,1)}, u32[]{:S(2)}) copy-start(bf16[2,128,128]{2,1,0:T(8,128)(2,1)} %get-tuple-element.31) | copy-start | bytes 196612
  52.8 26.2 %copy-start.15 = (bf16[2,128,128]{2,1,0:T(8,128)(2,1)S(1)}, bf16[2,128,128]{2,1,0:T(8,128)(2,1)}, u32[]{:S(2)}) copy-start(bf16[2,128,128]{2,1,0:T(8,128)(2,1)} %get-tuple-element.32) | copy-start | bytes 196612
  52.8 27.9 %copy-start.13 = (bf16[2,128,128]{2,1,0:T(8,128)(2,1)S(1)}, bf16[2,128,128]{2,1,0:T(8,128)(2,1)}, u32[]{:S(2)}) copy-start(bf16[2,128,128]{2,1,0:T(8,128)(2,1)} %get-tuple-element.33) | copy-start | bytes 196612
  52.9 29.6 %copy-start.12 = (bf16[2,128,128]{2,1,0:T(8,128)(2,1)S(1)}, bf16[2,128,128]{2,1,0:T(8,128)(2,1)}, u32[]{:S(2)}) copy-start(bf16[2,128,128]{2,1,0:T(8,128)(2,1)} %get-tuple-element.34) | copy-start | bytes 196612
  52.9 31.4 %copy-start.10 = (bf16[2,128,128]{2,1,0:T(8,128)(2,1)S(1)}, bf16[2,128,128]{2,1,0:T(8,128)(2,1)}, u32[]{:S(2)}) copy-start(bf16[2,128,128]{2,1,0:T(8,128)(2,1)} %get-tuple-element.35) | copy-start | bytes 196612
  52.9 50.8 %all-to-all-start.2 = ((bf16[16,128,128]{2,1,0:T(8,128)(2,1)}), bf16[16,128,128]{2,1,0:T(8,128)(2,1)S(1)}, u32[]{:S(2)}, u32[]{:S(2)}) async-start(bf16[16,128,128]{2,1,0:T(8,128)(2,1)} %get-tuple-element.42), calls=%async_computation.2 | async-start | bytes 1048576 | tf_op jit(solution)/shard_map/all_to_all | solution.py:302
  60.3 30.2 %copy-start.8 = (bf16[2,128,128]{2,1,0:T(8,128)(2,1)}, bf16[2,128,128]{2,1,0:T(8,128)(2,1)S(1)}, u32[]{:S(2)}) copy-start(bf16[2,128,128]{2,1,0:T(8,128)(2,1)S(1)} %collective-permute-done.refs_3_) | copy-start | bytes 196612
  60.4 14.6 %collective-permute-start.13 = (bf16[2,128,128]{2,1,0:T(8,128)(2,1)S(1)}, bf16[2,128,128]{2,1,0:T(8,128)(2,1)S(1)}, u32[]{:S(2)}, u32[]{:S(2)}) collective-permute-start(bf16[2,128,128]{2,1,0:T(8,128)(2,1)S(1)} %copy-done.24), channel_id=1, source_target_pairs={{0,14},{1,15},{2,12},{3,13},{4,10},{5,11},{6,8},{7,9},{8,6},{9,7},... | collective-permute-start | bytes 196616 | tf_op jit(solution)/shard_map/ppermute | solution.py:278
  65.0 25.5 %copy-start.9 = (bf16[2,128,128]{2,1,0:T(8,128)(2,1)}, bf16[2,128,128]{2,1,0:T(8,128)(2,1)S(1)}, u32[]{:S(2)}) copy-start(bf16[2,128,128]{2,1,0:T(8,128)(2,1)S(1)} %collective-permute-done.1.refs_4_) | copy-start | bytes 196612
  65.0 14.0 %collective-permute-start.14 = (bf16[2,128,128]{2,1,0:T(8,128)(2,1)S(1)}, bf16[2,128,128]{2,1,0:T(8,128)(2,1)S(1)}, u32[]{:S(2)}, u32[]{:S(2)}) collective-permute-start(bf16[2,128,128]{2,1,0:T(8,128)(2,1)S(1)} %copy-done.22), channel_id=1, source_target_pairs={{0,15},{1,14},{2,13},{3,12},{4,11},{5,10},{6,9},{7,8},{8,7},{9,6},... | collective-permute-start | bytes 196616 | tf_op jit(solution)/shard_map/ppermute | solution.py:278
  66.6 24.0 %copy-start.11 = (bf16[2,128,128]{2,1,0:T(8,128)(2,1)}, bf16[2,128,128]{2,1,0:T(8,128)(2,1)S(1)}, u32[]{:S(2)}) copy-start(bf16[2,128,128]{2,1,0:T(8,128)(2,1)S(1)} %collective-permute-done.10.refs_13_) | copy-start | bytes 196612
  66.6 14.1 %collective-permute-start.2 = (bf16[2,128,128]{2,1,0:T(8,128)(2,1)S(1)}, bf16[2,128,128]{2,1,0:T(8,128)(2,1)S(1)}, u32[]{:S(2)}, u32[]{:S(2)}) collective-permute-start(bf16[2,128,128]{2,1,0:T(8,128)(2,1)S(1)} %copy-done.20), channel_id=1, source_target_pairs={{0,3},{1,2},{2,1},{3,0},{4,7},{5,6},{6,5},{7,4},{8,11},{9,10},{10,... | collective-permute-start | bytes 196616 | tf_op jit(solution)/shard_map/ppermute | solution.py:278
  68.1 22.5 %copy-start.14 = (bf16[2,128,128]{2,1,0:T(8,128)(2,1)}, bf16[2,128,128]{2,1,0:T(8,128)(2,1)S(1)}, u32[]{:S(2)}) copy-start(bf16[2,128,128]{2,1,0:T(8,128)(2,1)S(1)} %collective-permute-done.11.refs_14_) | copy-start | bytes 196612
  68.1 14.3 %collective-permute-start.3 = (bf16[2,128,128]{2,1,0:T(8,128)(2,1)S(1)}, bf16[2,128,128]{2,1,0:T(8,128)(2,1)S(1)}, u32[]{:S(2)}, u32[]{:S(2)}) collective-permute-start(bf16[2,128,128]{2,1,0:T(8,128)(2,1)S(1)} %copy-done.19), channel_id=1, source_target_pairs={{0,4},{1,5},{2,6},{3,7},{4,0},{5,1},{6,2},{7,3},{8,12},{9,13},{10,... | collective-permute-start | bytes 196616 | tf_op jit(solution)/shard_map/ppermute | solution.py:278
  68.2 22.4 %copy-start.17 = (bf16[2,128,128]{2,1,0:T(8,128)(2,1)}, bf16[2,128,128]{2,1,0:T(8,128)(2,1)S(1)}, u32[]{:S(2)}) copy-start(bf16[2,128,128]{2,1,0:T(8,128)(2,1)S(1)} %collective-permute-done.12.refs_15_) | copy-start | bytes 196612
  68.2 16.1 %collective-permute-start.4 = (bf16[2,128,128]{2,1,0:T(8,128)(2,1)S(1)}, bf16[2,128,128]{2,1,0:T(8,128)(2,1)S(1)}, u32[]{:S(2)}, u32[]{:S(2)}) collective-permute-start(bf16[2,128,128]{2,1,0:T(8,128)(2,1)S(1)} %copy-done.18), channel_id=1, source_target_pairs={{0,5},{1,4},{2,7},{3,6},{4,1},{5,0},{6,3},{7,2},{8,13},{9,12},{10,... | collective-permute-start | bytes 196616 | tf_op jit(solution)/shard_map/ppermute | solution.py:278
  75.0 15.6 %copy-start.21 = (bf16[2,128,128]{2,1,0:T(8,128)(2,1)}, bf16[2,128,128]{2,1,0:T(8,128)(2,1)S(1)}, u32[]{:S(2)}) copy-start(bf16[2,128,128]{2,1,0:T(8,128)(2,1)S(1)} %collective-permute-done.13.refs_16_) | copy-start | bytes 196612
  75.0 10.6 %collective-permute-start.5 = (bf16[2,128,128]{2,1,0:T(8,128)(2,1)S(1)}, bf16[2,128,128]{2,1,0:T(8,128)(2,1)S(1)}, u32[]{:S(2)}, u32[]{:S(2)}) collective-permute-start(bf16[2,128,128]{2,1,0:T(8,128)(2,1)S(1)} %copy-done.16), channel_id=1, source_target_pairs={{0,6},{1,7},{2,4},{3,5},{4,2},{5,3},{6,0},{7,1},{8,14},{9,15},{10,... | collective-permute-start | bytes 196616 | tf_op jit(solution)/shard_map/ppermute | solution.py:278
  79.1 11.5 %copy-start.23 = (bf16[2,128,128]{2,1,0:T(8,128)(2,1)}, bf16[2,128,128]{2,1,0:T(8,128)(2,1)S(1)}, u32[]{:S(2)}) copy-start(bf16[2,128,128]{2,1,0:T(8,128)(2,1)S(1)} %collective-permute-done.14.refs_17_) | copy-start | bytes 196612
  79.1 7.1 %collective-permute-start.6 = (bf16[2,128,128]{2,1,0:T(8,128)(2,1)S(1)}, bf16[2,128,128]{2,1,0:T(8,128)(2,1)S(1)}, u32[]{:S(2)}, u32[]{:S(2)}) collective-permute-start(bf16[2,128,128]{2,1,0:T(8,128)(2,1)S(1)} %copy-done.15), channel_id=1, source_target_pairs={{0,7},{1,6},{2,5},{3,4},{4,3},{5,2},{6,1},{7,0},{8,15},{9,14},{10,... | collective-permute-start | bytes 196616 | tf_op jit(solution)/shard_map/ppermute | solution.py:278
  80.7 9.9 %copy-start.25 = (bf16[2,128,128]{2,1,0:T(8,128)(2,1)}, bf16[2,128,128]{2,1,0:T(8,128)(2,1)S(1)}, u32[]{:S(2)}) copy-start(bf16[2,128,128]{2,1,0:T(8,128)(2,1)S(1)} %collective-permute-done.2.refs_5_) | copy-start | bytes 196612
  80.7 5.7 %collective-permute-start.7 = (bf16[2,128,128]{2,1,0:T(8,128)(2,1)S(1)}, bf16[2,128,128]{2,1,0:T(8,128)(2,1)S(1)}, u32[]{:S(2)}, u32[]{:S(2)}) collective-permute-start(bf16[2,128,128]{2,1,0:T(8,128)(2,1)S(1)} %copy-done.13), channel_id=1, source_target_pairs={{0,8},{1,9},{2,10},{3,11},{4,12},{5,13},{6,14},{7,15},{8,0},{9,1},... | collective-permute-start | bytes 196616 | tf_op jit(solution)/shard_map/ppermute | solution.py:278
  82.4 8.2 %copy-start.26 = (bf16[2,128,128]{2,1,0:T(8,128)(2,1)}, bf16[2,128,128]{2,1,0:T(8,128)(2,1)S(1)}, u32[]{:S(2)}) copy-start(bf16[2,128,128]{2,1,0:T(8,128)(2,1)S(1)} %collective-permute-done.3.refs_6_) | copy-start | bytes 196612
  82.4 7.0 %collective-permute-start.8 = (bf16[2,128,128]{2,1,0:T(8,128)(2,1)S(1)}, bf16[2,128,128]{2,1,0:T(8,128)(2,1)S(1)}, u32[]{:S(2)}, u32[]{:S(2)}) collective-permute-start(bf16[2,128,128]{2,1,0:T(8,128)(2,1)S(1)} %copy-done.12), channel_id=1, source_target_pairs={{0,9},{1,8},{2,11},{3,10},{4,13},{5,12},{6,15},{7,14},{8,1},{9,0},... | collective-permute-start | bytes 196616 | tf_op jit(solution)/shard_map/ppermute | solution.py:278
  84.3 6.3 %copy-start.27 = (bf16[2,128,128]{2,1,0:T(8,128)(2,1)}, bf16[2,128,128]{2,1,0:T(8,128)(2,1)S(1)}, u32[]{:S(2)}) copy-start(bf16[2,128,128]{2,1,0:T(8,128)(2,1)S(1)} %collective-permute-done.4.refs_7_) | copy-start | bytes 196612
  84.3 6.2 %collective-permute-start.9 = (bf16[2,128,128]{2,1,0:T(8,128)(2,1)S(1)}, bf16[2,128,128]{2,1,0:T(8,128)(2,1)S(1)}, u32[]{:S(2)}, u32[]{:S(2)}) collective-permute-start(bf16[2,128,128]{2,1,0:T(8,128)(2,1)S(1)} %copy-done.10), channel_id=1, source_target_pairs={{0,10},{1,11},{2,8},{3,9},{4,14},{5,15},{6,12},{7,13},{8,2},{9,3},... | collective-permute-start | bytes 196616 | tf_op jit(solution)/shard_map/ppermute | solution.py:278
  85.6 5.1 %copy-start.28 = (bf16[2,128,128]{2,1,0:T(8,128)(2,1)}, bf16[2,128,128]{2,1,0:T(8,128)(2,1)S(1)}, u32[]{:S(2)}) copy-start(bf16[2,128,128]{2,1,0:T(8,128)(2,1)S(1)} %collective-permute-done.5.refs_8_) | copy-start | bytes 196612
  86.2 4.5 %copy-start.29 = (bf16[2,128,128]{2,1,0:T(8,128)(2,1)}, bf16[2,128,128]{2,1,0:T(8,128)(2,1)S(1)}, u32[]{:S(2)}) copy-start(bf16[2,128,128]{2,1,0:T(8,128)(2,1)S(1)} %collective-permute-done.6.refs_9_) | copy-start | bytes 196612
  86.4 4.2 %copy-start.30 = (bf16[2,128,128]{2,1,0:T(8,128)(2,1)}, bf16[2,128,128]{2,1,0:T(8,128)(2,1)S(1)}, u32[]{:S(2)}) copy-start(bf16[2,128,128]{2,1,0:T(8,128)(2,1)S(1)} %collective-permute-done.7.refs_10_) | copy-start | bytes 196612
  89.5 1.2 copy-start.31
  90.6 0.6 copy-start.32
  91.2 12.0 %copy-start.7 = (bf16[2,1024,128]{2,1,0:T(8,128)(2,1)S(1)}, bf16[2,1024,128]{2,1,0:T(8,128)(2,1)}, u32[]{:S(2)}) copy-start(bf16[2,1024,128]{2,1,0:T(8,128)(2,1)} %get-tuple-element.44) | copy-start | bytes 1572868
  103.1 5.5 %collective-permute-start.18 = (bf16[2,1024,128]{2,1,0:T(8,128)(2,1)}, bf16[2,1024,128]{2,1,0:T(8,128)(2,1)S(1)}, u32[]{:S(2)}, u32[]{:S(2)}) collective-permute-start(bf16[2,1024,128]{2,1,0:T(8,128)(2,1)} %get-tuple-element.46), channel_id=1, source_target_pairs={{0,16},{16,0},{1,17},{17,1},{2,18},{18,2},{3,19},{19,3},{4,20},{20... | collective-permute-start | bytes 1572872 | tf_op jit(solution)/shard_map/ppermute | solution.py:295
  103.2 5.6 %collective-permute-start.17 = (bf16[2,1024,128]{2,1,0:T(8,128)(2,1)S(1)}, bf16[2,1024,128]{2,1,0:T(8,128)(2,1)S(1)}, u32[]{:S(2)}, u32[]{:S(2)}) collective-permute-start(bf16[2,1024,128]{2,1,0:T(8,128)(2,1)S(1)} %copy-done.7), channel_id=1, source_target_pairs={{0,16},{16,0},{1,17},{17,1},{2,18},{18,2},{3,19},{19,3},{4,20},{20... | collective-permute-start | bytes 1572872 | tf_op jit(solution)/shard_map/ppermute | solution.py:295
  103.7 4.9 %copy-start.2 = (bf16[2,1024,128]{2,1,0:T(8,128)(2,1)S(1)}, bf16[2,1024,128]{2,1,0:T(8,128)(2,1)}, u32[]{:S(2)}) copy-start(bf16[2,1024,128]{2,1,0:T(8,128)(2,1)} %get-tuple-element.45) | copy-start | bytes 1572868
  103.7 20.2 %all-to-all-start = ((bf16[16,128,128]{2,1,0:T(8,128)(2,1)}), bf16[16,128,128]{2,1,0:T(8,128)(2,1)S(1)}, u32[]{:S(2)}, u32[]{:S(2)}) async-start(bf16[16,128,128]{2,1,0:T(8,128)(2,1)} %get-tuple-element.41), calls=%async_computation | async-start | bytes 1048576 | tf_op jit(solution)/shard_map/all_to_all | solution.py:302
  108.7 1.0 copy-start.1
